TPU v7x, 32 devices: a whole 2x2x4 slice. The times are simulated.
32 devices in a mesh: rep: 2 (over y), branch: 4 (over z), leaf: 4 (over x, core).
Axes of the slice: x: 2, y: 2, z: 4, core: 2. Of those that a mesh axis runs over, the one named last changes fastest.
Arguments:
- queries: bfloat16 [4096, 4096], P(('rep', 'branch', 'leaf')), parts along dimension 0, may hold values from -8 to 8
- leaf_kv: bfloat16 [4096, 1024], P(('rep', 'branch', 'leaf')), parts along dimension 0, may hold values from -6 to 6
- branch_kv: bfloat16 [8192, 1024], P(('rep', 'branch', 'leaf')), parts along dimension 0, may hold values from -6 to 6
- root_kv: bfloat16 [4096, 1024], P(('rep', 'branch', 'leaf')), parts along dimension 0, may hold values from -8 to 8
- branch_len: int32 [16], P('rep'), parts along dimension 0, may hold values from 1 to 512, 3072 in all
- leaf_len: int32 [32], P(('rep', 'branch', 'leaf')), parts along dimension 0, may hold values from 1 to 128, 1536 in all
- leaf_parent: int32 [32], P(('rep', 'branch', 'leaf')), parts along dimension 0, may hold values from 0 to 7, as said below
Outputs:
- attended: bfloat16 [4096, 4096], P(('rep', 'branch', 'leaf')), parts along dimension 0
There are 2 independent parts, one for each index of `rep`. A program takes and returns all parts, laid end to end along the dimension named above; each array names one. Nothing has to cross between parts.
Inputs may be any that keep to these rules, and one draw needn't show every extreme that they name: `leaf_parent`: leaf i's parent is one of the 2 branches of trunk i // 4, numbered from (i // 4) * 2; every branch is the parent of at least one leaf.
All inputs are finite; a program needn't handle non-finite values. No bound on the sum of `leaf_len` on one device may be relied on, other than what follows from the above.
Results may differ from a plain program's by a relative error of at most 0.005.
Values may be sent and summed in bfloat16 or wider, within the bound.
No kernel may reach another device: no remote copies, remote signals or barrier semaphores. Data moves between devices by JAX's collectives and lax.ppermute only.
A program may use at most 64 MiB of HBM per device.

v0:
```python
import jax
import jax.numpy as jnp
from jax import lax
from jax.sharding import PartitionSpec as P

QH = 32
KVH = 4
DH = 128
BR_DEV = 2
BL = 512


key_block = 256
neg_large = -1e30


def absorb(carried, query_rows, kv_piece, visible):
    running_max, denominator, numerator = carried
    kv_width = kv_piece.shape[1] // 2
    kv_heads = query_rows.shape[1]
    head_size = query_rows.shape[3]
    key_rows = kv_piece[:, :kv_width].reshape(kv_piece.shape[0], kv_heads, head_size)
    value_rows = kv_piece[:, kv_width:].reshape(kv_piece.shape[0], kv_heads, head_size)
    scores = jnp.einsum(
        "qkgd,tkd->qkgt", query_rows, key_rows, preferred_element_type=jnp.float32
    ) * head_size ** (-0.5)
    if visible is not None:
        scores = jnp.where(visible, scores, -jnp.inf)
    new_max = jnp.maximum(running_max, jnp.max(scores, axis=-1))
    rescale = jnp.exp(running_max - new_max)
    weights = jnp.exp(scores - new_max[..., None])
    denominator = denominator * rescale + jnp.sum(weights, axis=-1)
    product = jnp.einsum(
        "qkgt,tkd->qkgd",
        weights.astype(jnp.bfloat16),
        value_rows,
        preferred_element_type=jnp.float32,
    )
    numerator = numerator * rescale[..., None] + product
    return (new_max, denominator, numerator)


def absorb_span(carried, query_rows, kv_piece, key_limit):
    key_count = kv_piece.shape[0]
    block_count = key_count // key_block
    pieces = kv_piece.reshape(block_count, key_block, kv_piece.shape[1])
    starts = lax.iota(jnp.int32, block_count) * key_block

    def advance(state_now, element):
        block_kv, offset = element
        if key_limit is None:
            visible = None
        else:
            visible = (offset + lax.iota(jnp.int32, key_block) < key_limit)[None, None, None, :]
        return (absorb(state_now, query_rows, block_kv, visible), None)

    carried, unused = lax.scan(advance, carried, (pieces, starts))
    return carried


def body(queries, leaf_kv, branch_kv, root_kv, branch_len, leaf_len, leaf_parent):
    query_count = queries.shape[0]
    groups = QH // KVH
    query_rows = queries.reshape(query_count, KVH, groups, DH)
    trunk_rows = lax.all_gather(branch_kv, "leaf", axis=0, tiled=True)
    parent = leaf_parent[0]
    local_branch = parent - lax.axis_index("branch") * BR_DEV
    branch_rows = lax.dynamic_slice_in_dim(trunk_rows, local_branch * BL, BL, 0)
    carried = (
        jnp.full((query_count, KVH, groups), neg_large, jnp.float32),
        jnp.zeros((query_count, KVH, groups), jnp.float32),
        jnp.zeros((query_count, KVH, groups, DH), jnp.float32),
    )
    causal = lax.iota(jnp.int32, query_count)[None, :] <= lax.iota(jnp.int32, query_count)[:, None]
    carried = absorb(carried, query_rows, leaf_kv, causal[:, None, None, :])
    carried = absorb_span(carried, query_rows, branch_rows, branch_len[parent])
    whole_root = lax.all_gather(root_kv, ("branch", "leaf"), axis=0, tiled=True)
    carried = absorb_span(carried, query_rows, whole_root, None)
    running_max, denominator, numerator = carried
    output = (numerator / denominator[..., None]).reshape(query_count, QH * DH)
    live_rows = lax.iota(jnp.int32, query_count)[:, None] < leaf_len[0]
    output = jnp.where(live_rows, output, jnp.zeros_like(output))
    return output.astype(jnp.bfloat16)


def solution(mesh):
    placed = (
        P(("rep", "branch", "leaf"), None),
        P(("rep", "branch", "leaf"), None),
        P(("rep", "branch", "leaf"), None),
        P(("rep", "branch", "leaf"), None),
        P("rep"),
        P(("rep", "branch", "leaf")),
        P(("rep", "branch", "leaf")),
    )
    return jax.shard_map(
        body,
        mesh=mesh,
        in_specs=placed,
        out_specs=P(("rep", "branch", "leaf"), None),
        check_vma=False,
    )
```

profile of v0, /device:TPU:0, one launch (start us, length us, event | category | flops | bytes accessed | tf_op | source)
XLA Modules:
  0.0 159.5 jit_solution(13174131486892823722)
XLA Ops:
  11.6 2.0 %bitcast_add_fusion.2 = f32[128,4,8,128]{3,0,2,1:T(8,128)} fusion(bf16[128,4,128,1]{0,2,3,1:T(8,128)(2,1)S(1)} %bitcast.139, f32[128,4,8,128]{0,3,2,1:T(8,128)S(1)} %get-tuple-element.154, f32[128,4,8]{0,2,1:T(8,128)S(1)} %get-tuple-element.151, f32[128,4,8]{0,2,1:T(8,128)S(1)} %broadcast_maximum_fusion), kind=kOutput, calls=%fused_computation.31 | convolution fusion | flops 135790592 | bytes 4358144 | tf_op jit(solution)/shard_map/qkgt,tkd->qkgd/dot_general | solution.py:33
  13.6 1.9 %copy.24 = f32[128,4,8,128]{0,3,2,1:T(8,128)S(1)} copy(f32[128,4,8,128]{3,0,2,1:T(8,128)} %bitcast_add_fusion.2) | data formatting | bytes 4194304 | tf_op jit(solution)/shard_map/while | solution.py:57
  17.5 16.7 %all-gather.3.cloned.1.call-done = bf16[1024,1024]{1,0:T(8,128)(2,1)} async-done(((bf16[256,1024]{1,0:T(8,128)(2,1)}), bf16[1024,1024]{1,0:T(8,128)(2,1)}) %all-gather.3.cloned.1.call-update) | async-done | bytes 2097168 | tf_op jit(solution)/shard_map/all_gather | solution.py:65
  34.2 2.3 %constant_dynamic-slice_fusion.2 = bf16[512,1024]{1,0:T(8,128)(2,1)} fusion(bf16[1024,1024]{1,0:T(8,128)(2,1)} %all-gather.3.cloned.1.call-done, s32[]{:T(128)S(6)} %select_n.23), kind=kLoop, calls=%fused_computation.44 | loop fusion | bytes 2097156 | tf_op jit(solution)/shard_map/dynamic_slice | solution.py:68
  36.5 21.2 %while.28 = (s32[]{:T(128)}, f32[128,4,8]{0,2,1:T(8,128)S(1)}, f32[128,4,8]{0,2,1:T(8,128)S(1)}, f32[128,4,8,128]{0,3,2,1:T(8,128)S(1)}, s32[2]{0:T(128)S(1)}, /...) while((s32[]{:T(128)}, f32[128,4,8]{0,2,1:T(8,128)S(1)}, ...), condition=%wide.region_5.6_spmd, body=%wide.region_2.5_spmd.sunk | while | flops 549462528 | bytes 21759092 | solution.py:57
  38.5 1.9 %constant_dynamic-slice_fusion.5 = bf16[1,256,1024]{2,1,0:T(8,128)(2,1)} fusion(bf16[2,256,1024]{2,1,0:T(8,128)(2,1)} %get-tuple-element.289, s32[]{:T(128)} %get-tuple-element.274), kind=kLoop, calls=%fused_computation.15.clone.1 | loop fusion | bytes 1048580 | tf_op jit(solution)/shard_map/while/body/jit(dynamic_index_in_dim)/dynamic_slice | solution.py:57
  40.3 2.1 %copy.55 = bf16[1,256,1024]{1,2,0:T(8,128)(2,1)} copy(bf16[1,256,1024]{2,1,0:T(8,128)(2,1)} %constant_dynamic-slice_fusion.5) | data formatting | bytes 1048576 | tf_op jit(solution)/shard_map/while/body/jit(dynamic_index_in_dim)/dynamic_slice | solution.py:57
  49.1 1.9 %constant_dynamic-slice_fusion.5 = bf16[1,256,1024]{2,1,0:T(8,128)(2,1)} fusion(bf16[2,256,1024]{2,1,0:T(8,128)(2,1)} %get-tuple-element.289, s32[]{:T(128)} %get-tuple-element.274), kind=kLoop, calls=%fused_computation.15.clone.1 | loop fusion | bytes 1048580 | tf_op jit(solution)/shard_map/while/body/jit(dynamic_index_in_dim)/dynamic_slice | solution.py:57
  50.9 2.1 %copy.55 = bf16[1,256,1024]{1,2,0:T(8,128)(2,1)} copy(bf16[1,256,1024]{2,1,0:T(8,128)(2,1)} %constant_dynamic-slice_fusion.5) | data formatting | bytes 1048576 | tf_op jit(solution)/shard_map/while/body/jit(dynamic_index_in_dim)/dynamic_slice | solution.py:57
  57.6 29.1 %all-gather.5.cloned.1.call-done = bf16[2048,1024]{1,0:T(8,128)(2,1)} async-done(((bf16[128,1024]{1,0:T(8,128)(2,1)}), bf16[2048,1024]{1,0:T(8,128)(2,1)}) %all-gather.5.cloned.1.call-update) | async-done | bytes 4194320 | tf_op jit(solution)/shard_map/all_gather | solution.py:77
  86.8 63.9 %while.29 = (s32[]{:T(128)}, f32[128,4,8]{0,2,1:T(8,128)S(1)}, f32[128,4,8]{0,2,1:T(8,128)S(1)}, f32[128,4,8,128]{0,3,2,1:T(8,128)S(1)}, bf16[8,256,1024]{2,1,0:...) while((s32[]{:T(128)}, f32[128,4,8]{0,2,1:T(8,128)S(1)}, f32[128,4,8]{0,2,1:T(8,128)S(1)}, ...), condition=%wide.region_9.10_spmd, body=%wide.region_6.9_spmd.sunk | while | flops 546316288 | bytes 21758032 | solution.py:57
  88.6 2.0 %copy.56 = bf16[1,256,1024]{1,2,0:T(8,128)(2,1)} copy(bf16[1,256,1024]{2,1,0:T(8,128)(2,1)} %constant_dynamic-slice_fusion.6) | data formatting | bytes 1048576 | tf_op jit(solution)/shard_map/while/body/jit(dynamic_index_in_dim)/dynamic_slice | solution.py:57
  94.7 1.9 %constant_dynamic-slice_fusion.6 = bf16[1,256,1024]{2,1,0:T(8,128)(2,1)} fusion(bf16[8,256,1024]{2,1,0:T(8,128)(2,1)} %get-tuple-element.310, s32[]{:T(128)} %get-tuple-element.299), kind=kLoop, calls=%fused_computation.29.clone.1 | loop fusion | bytes 1048580 | tf_op jit(solution)/shard_map/while/body/jit(dynamic_index_in_dim)/dynamic_slice | solution.py:57
  96.6 2.0 %copy.56 = bf16[1,256,1024]{1,2,0:T(8,128)(2,1)} copy(bf16[1,256,1024]{2,1,0:T(8,128)(2,1)} %constant_dynamic-slice_fusion.6) | data formatting | bytes 1048576 | tf_op jit(solution)/shard_map/while/body/jit(dynamic_index_in_dim)/dynamic_slice | solution.py:57
  102.7 1.9 %constant_dynamic-slice_fusion.6 = bf16[1,256,1024]{2,1,0:T(8,128)(2,1)} fusion(bf16[8,256,1024]{2,1,0:T(8,128)(2,1)} %get-tuple-element.310, s32[]{:T(128)} %get-tuple-element.299), kind=kLoop, calls=%fused_computation.29.clone.1 | loop fusion | bytes 1048580 | tf_op jit(solution)/shard_map/while/body/jit(dynamic_index_in_dim)/dynamic_slice | solution.py:57
  104.6 2.0 %copy.56 = bf16[1,256,1024]{1,2,0:T(8,128)(2,1)} copy(bf16[1,256,1024]{2,1,0:T(8,128)(2,1)} %constant_dynamic-slice_fusion.6) | data formatting | bytes 1048576 | tf_op jit(solution)/shard_map/while/body/jit(dynamic_index_in_dim)/dynamic_slice | solution.py:57
  110.7 1.9 %constant_dynamic-slice_fusion.6 = bf16[1,256,1024]{2,1,0:T(8,128)(2,1)} fusion(bf16[8,256,1024]{2,1,0:T(8,128)(2,1)} %get-tuple-element.310, s32[]{:T(128)} %get-tuple-element.299), kind=kLoop, calls=%fused_computation.29.clone.1 | loop fusion | bytes 1048580 | tf_op jit(solution)/shard_map/while/body/jit(dynamic_index_in_dim)/dynamic_slice | solution.py:57
  112.6 2.0 %copy.56 = bf16[1,256,1024]{1,2,0:T(8,128)(2,1)} copy(bf16[1,256,1024]{2,1,0:T(8,128)(2,1)} %constant_dynamic-slice_fusion.6) | data formatting | bytes 1048576 | tf_op jit(solution)/shard_map/while/body/jit(dynamic_index_in_dim)/dynamic_slice | solution.py:57
  118.7 1.9 %constant_dynamic-slice_fusion.6 = bf16[1,256,1024]{2,1,0:T(8,128)(2,1)} fusion(bf16[8,256,1024]{2,1,0:T(8,128)(2,1)} %get-tuple-element.310, s32[]{:T(128)} %get-tuple-element.299), kind=kLoop, calls=%fused_computation.29.clone.1 | loop fusion | bytes 1048580 | tf_op jit(solution)/shard_map/while/body/jit(dynamic_index_in_dim)/dynamic_slice | solution.py:57
  120.6 2.0 %copy.56 = bf16[1,256,1024]{1,2,0:T(8,128)(2,1)} copy(bf16[1,256,1024]{2,1,0:T(8,128)(2,1)} %constant_dynamic-slice_fusion.6) | data formatting | bytes 1048576 | tf_op jit(solution)/shard_map/while/body/jit(dynamic_index_in_dim)/dynamic_slice | solution.py:57
  128.6 2.0 %copy.56 = bf16[1,256,1024]{1,2,0:T(8,128)(2,1)} copy(bf16[1,256,1024]{2,1,0:T(8,128)(2,1)} %constant_dynamic-slice_fusion.6) | data formatting | bytes 1048576 | tf_op jit(solution)/shard_map/while/body/jit(dynamic_index_in_dim)/dynamic_slice | solution.py:57
  134.7 1.9 %constant_dynamic-slice_fusion.6 = bf16[1,256,1024]{2,1,0:T(8,128)(2,1)} fusion(bf16[8,256,1024]{2,1,0:T(8,128)(2,1)} %get-tuple-element.310, s32[]{:T(128)} %get-tuple-element.299), kind=kLoop, calls=%fused_computation.29.clone.1 | loop fusion | bytes 1048580 | tf_op jit(solution)/shard_map/while/body/jit(dynamic_index_in_dim)/dynamic_slice | solution.py:57
  136.6 2.0 %copy.56 = bf16[1,256,1024]{1,2,0:T(8,128)(2,1)} copy(bf16[1,256,1024]{2,1,0:T(8,128)(2,1)} %constant_dynamic-slice_fusion.6) | data formatting | bytes 1048576 | tf_op jit(solution)/shard_map/while/body/jit(dynamic_index_in_dim)/dynamic_slice | solution.py:57
  144.5 2.0 %copy.56 = bf16[1,256,1024]{1,2,0:T(8,128)(2,1)} copy(bf16[1,256,1024]{2,1,0:T(8,128)(2,1)} %constant_dynamic-slice_fusion.6) | data formatting | bytes 1048576 | tf_op jit(solution)/shard_map/while/body/jit(dynamic_index_in_dim)/dynamic_slice | solution.py:57
  (101 shorter events, 58.5 us)
Async XLA Ops:
  6.5 3.1 %copy-start = (bf16[128,1024]{1,0:T(8,128)(2,1)S(1)}, bf16[128,1024]{1,0:T(8,128)(2,1)}, u32[]{:S(2)}) copy-start(bf16[128,1024]{1,0:T(8,128)(2,1)} %param.12) | copy-start | bytes 786436
  6.5 27.7 %all-gather.3.cloned.1.call-start = ((), (), s32[]{:S(2)}) async-start(), calls=%async_computation | async-start | bytes 2621440 | tf_op jit(solution)/shard_map/all_gather | solution.py:65
  7.3 79.5 %all-gather.5.cloned.1.call-start = ((), (), s32[]{:S(2)}) async-start(), calls=%async_computation.1 | async-start | bytes 4456448 | tf_op jit(solution)/shard_map/all_gather | solution.py:77
  13.6 3.3 %copy-start.1 = (s32[8]{0:T(128)S(1)}, s32[8]{0:T(128)}, u32[]{:S(2)}) copy-start(s32[8]{0:T(128)} %param.15) | copy-start | bytes 100
Sparse Core Ops, SparseCore 0:
  8.9 25.2 all-gather.2
  36.4 50.3 all-gather.4
where the time goes:
time: 161 us; the launch traced here: 160 us
  local copies, waits for them, and re-layouts  59.1 us (37%)
  waiting for transfers between devices  47.3 us (29%)
  matrix products  24.8 us (15%)
  between operations  14.8 us (9%)
  other arithmetic  12.9 us (8%)
    dynamic_slice x22, local copies, waits for them, and re-layouts, absorb_span(): carried, unused = lax.scan(advance, carried, (pieces, starts))  40.5 us
    all_gather x1, waiting for transfers between devices, body(): whole_root = lax.all_gather(root_kv, ('branch', 'leaf'), axis=0, tiled=True)  29.1 us
    all_gather x1, waiting for transfers between devices, body(): trunk_rows = lax.all_gather(branch_kv, 'leaf', axis=0, tiled=True)  16.7 us
    dot_general x11, matrix products, absorb(): jnp.einsum('qkgt,tkd->qkgd', weights.astype(jnp.bfloat16), value_rows, pr...  16 us
    slice x11, local copies, waits for them, and re-layouts, absorb(): kv_piece[:, kv_width:].reshape(kv_piece.shape[0], kv_heads, head_size)  10.7 us
    dot_general x11, matrix products, absorb(): jnp.einsum('qkgd,tkd->qkgt', query_rows, key_rows, preferred_element_type...  8.86 us
    reduce_sum x11, other arithmetic, absorb(): denominator = denominator * rescale + jnp.sum(weights, axis=-1)  8.54 us
  transfers between devices with their start and end apart: 2, of which 2 were waited for; matrix products, arithmetic and copies ran while one was open for 20% of the time, Pallas kernels for 0%

commit v1 on v0

v1 whole, which is shorter than its diff:
```python
import functools
import math

import jax
import jax.numpy as jnp
from jax import lax
from jax.experimental import pallas as pl
from jax.experimental.pallas import tpu as pltpu
from jax.sharding import PartitionSpec as P

QH = 32
KVH = 4
DH = 128
BR_DEV = 2
BL = 512

neg_large = -1e30
key_tile = 256


def attend_kernel(kinds, table, query_ref, *refs):
    out_ref = refs[-1]
    row_count = query_ref.shape[0]
    groups = query_ref.shape[1] // DH
    total_rows = row_count * groups
    factor = DH ** -0.5 * math.log2(math.e)
    query = jnp.concatenate([query_ref[:, g * DH:(g + 1) * DH] for g in range(groups)], axis=0)
    row_max = jnp.full((total_rows, 1), neg_large, jnp.float32)
    total = None
    for number, kind in enumerate(kinds):
        key_ref, value_ref = refs[2 * number], refs[2 * number + 1]
        key_count = key_ref.shape[0]
        for start in range(0, key_count, key_tile):
            size = min(key_tile, key_count - start)
            keys = key_ref[start:start + size, :]
            values = value_ref[start:start + size, :]
            scores = lax.dot_general(
                query, keys, (((1,), (1,)), ((), ())), preferred_element_type=jnp.float32
            )
            if kind != "root":
                column = lax.broadcasted_iota(jnp.int32, scores.shape, 1) + start
                if kind == "leaf":
                    row = lax.rem(lax.broadcasted_iota(jnp.int32, scores.shape, 0), row_count)
                    visible = column <= row
                else:
                    visible = column < table[1]
                scores = jnp.where(visible, scores, neg_large)
            new_max = jnp.maximum(row_max, jnp.max(scores, axis=1, keepdims=True))
            weights = jnp.exp2((scores - new_max) * factor).astype(jnp.bfloat16)
            padded = jnp.concatenate([values, jnp.ones_like(values)], axis=1)
            product = jnp.dot(weights, padded, preferred_element_type=jnp.float32)
            if total is None:
                total = product
            else:
                total = total * jnp.exp2((row_max - new_max) * factor) + product
            row_max = new_max
    result = total[:, :DH] / total[:, DH:]
    live = lax.broadcasted_iota(jnp.int32, (row_count, DH), 0) < table[2]
    for g in range(groups):
        piece = result[g * row_count:(g + 1) * row_count]
        out_ref[:, g * DH:(g + 1) * DH] = jnp.where(live, piece, 0.0).astype(out_ref.dtype)


def attend(table, queries, leaf_rows, trunk_rows, root_rows):
    row_count = queries.shape[0]
    groups = QH // KVH
    query_spec = pl.BlockSpec((row_count, groups * DH), lambda k, t: (0, k))
    in_specs = [query_spec]
    operands = [queries]
    kinds = []
    for kind, rows, block in (("leaf", leaf_rows, None), ("branch", trunk_rows, BL), ("root", root_rows, None)):
        height = rows.shape[0] if block is None else block
        for offset in (0, KVH):
            if kind == "branch":
                spec = pl.BlockSpec((height, DH), lambda k, t, offset=offset: (t[0], k + offset))
            else:
                spec = pl.BlockSpec((height, DH), lambda k, t, offset=offset: (0, k + offset))
            in_specs.append(spec)
            operands.append(rows)
        kinds.append(kind)
    return pl.pallas_call(
        functools.partial(attend_kernel, tuple(kinds)),
        grid_spec=pltpu.PrefetchScalarGridSpec(
            num_scalar_prefetch=1, grid=(KVH,), in_specs=in_specs, out_specs=query_spec
        ),
        out_shape=jax.ShapeDtypeStruct(queries.shape, queries.dtype),
        compiler_params=pltpu.CompilerParams(vmem_limit_bytes=60 * 1024 * 1024),
        name="attend",
    )(table, *operands)


def body(queries, leaf_kv, branch_kv, root_kv, branch_len, leaf_len, leaf_parent):
    trunk_rows = lax.all_gather(branch_kv, "leaf", axis=0, tiled=True)
    whole_root = lax.all_gather(root_kv, ("branch", "leaf"), axis=0, tiled=True)
    parent = leaf_parent[0]
    local_branch = parent - lax.axis_index("branch") * BR_DEV
    table = jnp.stack([local_branch, branch_len[parent], leaf_len[0]])
    return attend(table, queries, leaf_kv, trunk_rows, whole_root)


def solution(mesh):
    split = P(("rep", "branch", "leaf"), None)
    single = P(("rep", "branch", "leaf"))
    return jax.shard_map(
        body,
        mesh=mesh,
        in_specs=(split, split, split, split, P("rep"), single, single),
        out_specs=split,
        check_vma=False,
    )
```

time: 161 us -> 112 us (0.70)
  local copies, waits for them, and re-layouts: 59.1 us -> 1.24 us
  waiting for transfers between devices: 47.3 us -> 76.3 us
  matrix products: 24.8 us -> 0 us
  Pallas kernels: 0 us -> 17.9 us
  other arithmetic: 12.9 us -> 1.29 us
    dynamic_slice x24 -> x1, local copies, waits for them, and re-layouts: 43.4 us -> 1.24 us  [body(): table = jnp.stack([local_branch, branch_len[parent], leaf_len[0]])]
    dot_general x22 -> x0, matrix products: 24.8 us -> none  [the longest x11 16 us: absorb(): jnp.einsum('qkgt,tkd->qkgd', weights.astype(jnp.bfloat16), value_rows, pr...]
    all_gather x1, waiting for transfers between devices: 29.1 us -> 52.6 us  [body(): whole_root = lax.all_gather(root_kv, ('branch', 'leaf'), axis=0, tiled=True)]
    pallas_call x0 -> x1, Pallas kernels: none -> 17.9 us  [attend(): pl.pallas_call(functools.partial(attend_kernel, tuple(kinds)), grid_spec=...]
    slice x11 -> x0, local copies, waits for them, and re-layouts: 10.7 us -> none  [absorb(): kv_piece[:, kv_width:].reshape(kv_piece.shape[0], kv_heads, head_size)]
    reduce_sum x11 -> x0, other arithmetic: 8.54 us -> none  [absorb(): denominator = denominator * rescale + jnp.sum(weights, axis=-1)]
    all_gather x1, waiting for transfers between devices: 16.7 us -> 22.4 us  [body(): trunk_rows = lax.all_gather(branch_kv, 'leaf', axis=0, tiled=True)]
    lt x3 -> x0, other arithmetic: 2.66 us -> none  [the longest x2 2.65 us: advance(): offset + lax.iota(jnp.int32, key_block) < key_limit]
  transfers between devices with their start and end apart: 2 -> 2, of which waited for: 2 -> 2; matrix products, arithmetic and copies ran while one was open for 20% -> 2% of each run, Pallas kernels for 0% -> 0%
where the time goes in v1:
time: 112 us; the launch traced here: 111 us
  waiting for transfers between devices  76.3 us (68%)
  Pallas kernels  17.9 us (16%)
  between operations  14.7 us (13%)
  other arithmetic  1.29 us (1%)
  local copies, waits for them, and re-layouts  1.24 us (1%)
    all_gather x1, waiting for transfers between devices, body(): whole_root = lax.all_gather(root_kv, ('branch', 'leaf'), axis=0, tiled=True)  52.6 us
    all_gather x1, waiting for transfers between devices, body(): trunk_rows = lax.all_gather(branch_kv, 'leaf', axis=0, tiled=True)  22.4 us
    pallas_call x1, Pallas kernels, attend(): pl.pallas_call(functools.partial(attend_kernel, tuple(kinds)), grid_spec=...  17.9 us
  transfers between devices with their start and end apart: 2, of which 2 were waited for; matrix products, arithmetic and copies ran while one was open for 2% of the time, Pallas kernels for 0%

profile of v1, /device:TPU:0, one launch (start us, length us, event | category | flops | bytes accessed | tf_op | source)
XLA Modules:
  0.0 111.5 jit_solution(14377439783260310416)
XLA Ops:
  6.5 0.0 all-gather.3.cloned.1.call-start
  6.5 0.7 all-gather.3.cloned.1.call-update
  7.3 0.0 all-gather.5.cloned.1.call-start
  7.3 0.7 all-gather.5.cloned.1.call-update
  9.3 1.2 %dynamic_slice.3 = s32[1]{0:T(128)} dynamic-slice(s32[8]{0:T(128)} %param.11, s32[]{:T(128)S(6)} %select_n.3), dynamic_slice_sizes={1} | dynamic-slice | bytes 12 | tf_op jit(solution)/shard_map/dynamic_slice | solution.py:97
  10.6 1.3 %pad_add_fusion.table = s32[3]{0:T(128)} fusion(s32[1]{0:T(128)S(6)} %copy.8, s32[1]{0:T(128)} %dynamic_slice.3, s32[1]{0:T(128)} %bitcast.1), kind=kLoop, calls=%fused_computation | loop fusion | flops 6 | bytes 24 | tf_op jit(solution)/shard_map/stack | solution.py:97
  11.8 22.4 %all-gather.3.cloned.1.call-done.refs_2_.refs_3_ = bf16[1024,1024]{1,0:T(8,128)(2,1)} async-done(((bf16[256,1024]{1,0:T(8,128)(2,1)}), bf16[1024,1024]{1,0:T(8,128)(2,1)}) %all-gather.3.cloned.1.call-update) | async-done | bytes 2097168 | tf_op jit(solution)/shard_map/all_gather | solution.py:93
  34.2 52.6 %all-gather.5.cloned.1.call-done.refs_4_.refs_5_ = bf16[2048,1024]{1,0:T(8,128)(2,1)} async-done(((bf16[128,1024]{1,0:T(8,128)(2,1)}), bf16[2048,1024]{1,0:T(8,128)(2,1)}) %all-gather.5.cloned.1.call-update) | async-done | bytes 4194320 | tf_op jit(solution)/shard_map/all_gather | solution.py:94
  86.8 17.9 %attend.1 = bf16[128,4096]{1,0:T(8,128)(2,1)} custom-call(s32[3]{0:T(128)} %pad_add_fusion.table, bf16[128,4096]{1,0:T(8,128)(2,1)} %query_ref.1, bf16[128,1024]{1,0:T(8,128)(2,1)} %refs_1_.1, bf16[128,1024]{1,0:T(8,128)(2,1)} %refs_1_.1, bf16[1024,1024]{1,0:T(8,128)(2,1)} %all-gather.3.cloned.1.call-done.refs_2_.refs_3_, ...), custom_call_target="tpu_custom_call" | custom-call | tf_op jit(solution)/shard_map/attend/pallas_call | solution.py:81
Async XLA Ops:
  6.5 27.7 %all-gather.3.cloned.1.call-start = ((), (), s32[]{:S(2)}) async-start(), calls=%async_computation | async-start | bytes 2621440 | tf_op jit(solution)/shard_map/all_gather | solution.py:93
  7.3 79.5 %all-gather.5.cloned.1.call-start = ((), (), s32[]{:S(2)}) async-start(), calls=%async_computation.1 | async-start | bytes 4456448 | tf_op jit(solution)/shard_map/all_gather | solution.py:94
Sparse Core Ops, SparseCore 0:
  8.9 25.2 all-gather.2
  36.4 50.3 all-gather.4

commit v2 on v1

v2 whole, which is shorter than its diff:
```python
import functools
import math

import jax
import jax.numpy as jnp
from jax import lax
from jax.experimental import pallas as pl
from jax.experimental.pallas import tpu as pltpu
from jax.sharding import PartitionSpec as P


QH = 32
KVH = 4
DH = 128
BR_DEV = 2
BL = 512


neg_large = -1e30
key_tile = 256
kernel_vmem = 24 * 1024 * 1024


def load_tile(pieces, refs, start, size):
    parts = []
    first = 0
    for number, height in pieces:
        low, high = max(start, first), min(start + size, first + height)
        if low < high:
            parts.append(refs[number][low - first:high - first, :])
        first += height
    return parts[0] if len(parts) == 1 else jnp.concatenate(parts, axis=0)


def attend_kernel(spans, carries, finishes, table, query_ref, *refs):
    row_count = query_ref.shape[0]
    groups = query_ref.shape[1] // DH
    total_rows = row_count * groups
    factor = DH ** -0.5 * math.log2(math.e)
    operand_count = 2 * sum(len(pieces) for kind, pieces in spans)
    key_refs = refs[:operand_count:2]
    value_refs = refs[1:operand_count:2]
    rest = refs[operand_count:]
    query = jnp.concatenate([query_ref[:, g * DH:(g + 1) * DH] for g in range(groups)], axis=0)
    if carries:
        total = jnp.concatenate([rest[0][...], jnp.ones((total_rows, DH), jnp.float32)], axis=1)
        row_max = jnp.max(rest[1][...], axis=1, keepdims=True)
        rest = rest[2:]
    else:
        row_max = jnp.full((total_rows, 1), neg_large, jnp.float32)
        total = None
    for kind, pieces in spans:
        key_count = sum(height for number, height in pieces)
        for start in range(0, key_count, key_tile):
            size = min(key_tile, key_count - start)
            keys = load_tile(pieces, key_refs, start, size)
            values = load_tile(pieces, value_refs, start, size)
            scores = lax.dot_general(
                query, keys, (((1,), (1,)), ((), ())), preferred_element_type=jnp.float32
            )
            if kind != "root":
                column = lax.broadcasted_iota(jnp.int32, scores.shape, 1) + start
                if kind == "leaf":
                    row = lax.rem(lax.broadcasted_iota(jnp.int32, scores.shape, 0), row_count)
                    visible = column <= row
                else:
                    visible = column < table[1]
                scores = jnp.where(visible, scores, neg_large)
            new_max = jnp.maximum(row_max, jnp.max(scores, axis=1, keepdims=True))
            weights = jnp.exp2((scores - new_max) * factor).astype(jnp.bfloat16)
            padded = jnp.concatenate([values, jnp.ones_like(values)], axis=1)
            product = jnp.dot(weights, padded, preferred_element_type=jnp.float32)
            if total is None:
                total = product
            else:
                total = total * jnp.exp2((row_max - new_max) * factor) + product
            row_max = new_max
    result = total[:, :DH] / total[:, DH:]
    if finishes:
        out_ref = rest[0]
        live = lax.broadcasted_iota(jnp.int32, (row_count, DH), 0) < table[2]
        for g in range(groups):
            piece = result[g * row_count:(g + 1) * row_count]
            out_ref[:, g * DH:(g + 1) * DH] = jnp.where(live, piece, 0.0).astype(out_ref.dtype)
    else:
        rest[0][...] = result
        rest[1][...] = row_max + jnp.log2(total[:, DH:]) * (1.0 / factor)


def attend(table, queries, spans, state=None, finishes=False):
    row_count = queries.shape[0]
    groups = QH // KVH
    query_spec = pl.BlockSpec((row_count, groups * DH), lambda k, t: (0, k))
    state_spec = pl.BlockSpec((row_count * groups, DH), lambda k, t: (k, 0))
    in_specs, operands, described = [query_spec], [queries], []
    number = 0
    key_count = 0
    for kind, pieces in spans:
        listed = []
        for rows, block in pieces:
            height = rows.shape[0] if block is None else block
            for offset in (0, KVH):
                if block is None:
                    index = lambda k, t, offset=offset: (0, k + offset)
                else:
                    index = lambda k, t, offset=offset: (t[0], k + offset)
                in_specs.append(pl.BlockSpec((height, DH), index))
                operands.append(rows)
            listed.append((number, height))
            number += 1
            key_count += height
        described.append((kind, tuple(listed)))
    if state is not None:
        in_specs.extend((state_spec, state_spec))
        operands.extend(state)
    if finishes:
        out_specs = query_spec
        out_shape = jax.ShapeDtypeStruct(queries.shape, queries.dtype)
    else:
        out_specs = (state_spec, state_spec)
        part = jax.ShapeDtypeStruct((KVH * row_count * groups, DH), jnp.float32)
        out_shape = (part, part)
    return pl.pallas_call(
        functools.partial(attend_kernel, tuple(described), state is not None, finishes),
        grid_spec=pltpu.PrefetchScalarGridSpec(
            num_scalar_prefetch=1, grid=(KVH,), in_specs=in_specs, out_specs=out_specs
        ),
        out_shape=out_shape,
        compiler_params=pltpu.CompilerParams(vmem_limit_bytes=kernel_vmem),
        cost_estimate=pl.CostEstimate(
            flops=4 * row_count * QH * DH * key_count,
            bytes_accessed=2 * row_count * QH * DH * 4,
            transcendentals=row_count * QH * key_count,
        ),
    )(table, *operands)


def gathered_body(queries, leaf_kv, branch_kv, root_kv, branch_len, leaf_len, leaf_parent):
    trunk_rows = lax.all_gather(branch_kv, "leaf", axis=0, tiled=True)
    whole_root = lax.all_gather(root_kv, ("branch", "leaf"), axis=0, tiled=True)
    parent = leaf_parent[0]
    local_branch = parent - lax.axis_index("branch") * BR_DEV
    table = jnp.stack([local_branch, branch_len[parent], leaf_len[0]])
    spans = [("leaf", [(leaf_kv, None)]), ("branch", [(trunk_rows, BL)]), ("root", [(whole_root, None)])]
    return attend(table, queries, spans, finishes=True)


def exchanged_body(queries, leaf_kv, branch_kv, root_kv, branch_len, leaf_len, leaf_parent):
    across = [(i, i ^ 2) for i in range(4)]
    beside = [(i, i ^ 1) for i in range(4)]
    near = [(i, i ^ 1) for i in range(4)]
    far = [(i, i ^ 3) for i in range(4)]
    cross = [(1, 0), (2, 3), (3, 1), (0, 2)]

    def swap(rows):
        return lax.ppermute(rows, "leaf", beside)

    z = lax.axis_index("branch")
    at_end = (z == 0) | (z == 3)
    parent = leaf_parent[0]
    local_branch = parent - z * BR_DEV
    place = lax.axis_index("leaf")
    elsewhere = local_branch != place // 2
    table = jnp.stack([jnp.int32(0), branch_len[parent], leaf_len[0]])

    own = root_kv
    far_own = lax.ppermute(own, "branch", far)
    near_own = lax.ppermute(own, "branch", near)
    side = lax.ppermute(own, "leaf", across)
    branch_side = lax.ppermute(branch_kv, "leaf", across)
    own_swapped = swap(own)
    branch_swapped = swap(branch_kv)
    state = attend(table, queries, [("leaf", [(leaf_kv, None)]), ("root", [(own, None), (own_swapped, None)])])

    cross_own = lax.ppermute(jnp.where(at_end, own, far_own), "branch", cross)
    near_side = lax.ppermute(side, "branch", near)
    far_side = lax.ppermute(far_own, "leaf", across)
    side_swapped = swap(side)
    near_own_swapped = swap(near_own)
    far_own_swapped = swap(far_own)
    branch_side_swapped = swap(branch_side)
    held = jnp.where(elsewhere, branch_side, branch_kv)
    swapped = jnp.where(elsewhere, branch_side_swapped, branch_swapped)
    first = place % 2 == 0
    low = jnp.where(first, held, swapped)
    high = jnp.where(first, swapped, held)
    state = attend(table, queries, [
        ("root", [(rows, None) for rows in (
            side, side_swapped, near_own, near_own_swapped, far_own, far_own_swapped)]),
        ("branch", [(low, None), (high, None)]),
    ], state)

    cross_side = lax.ppermute(jnp.where(at_end, side, far_side), "branch", cross)
    near_side_swapped = swap(near_side)
    far_side_swapped = swap(far_side)
    cross_own_swapped = swap(cross_own)
    state = attend(table, queries, [
        ("root", [(rows, None) for rows in (
            near_side, near_side_swapped, far_side, far_side_swapped, cross_own, cross_own_swapped)]),
    ], state)
    cross_side_swapped = swap(cross_side)
    return attend(table, queries, [("root", [(cross_side, None), (cross_side_swapped, None)])], state, finishes=True)


def solution(mesh):
    split = P(("rep", "branch", "leaf"), None)
    single = P(("rep", "branch", "leaf"))
    small = mesh.shape["branch"] == 4 and mesh.shape["leaf"] == 4
    return jax.shard_map(
        exchanged_body if small else gathered_body,
        mesh=mesh,
        in_specs=(split, split, split, split, P("rep"), single, single),
        out_specs=split,
        check_vma=False,
    )
```

time: 112 us -> 65.8 us (0.59)
  waiting for transfers between devices: 76.3 us -> 16.1 us
  starting transfers between devices: 0.04 us -> 16.5 us
  between operations: 14.7 us -> 1.42 us
  Pallas kernels: 17.9 us -> 25.2 us
  local copies, waits for them, and re-layouts: 1.24 us -> 4.45 us
    all_gather x2 -> x0, waiting for transfers between devices: 74.9 us -> none  [the longest x1 52.6 us: body(): whole_root = lax.all_gather(root_kv, ('branch', 'leaf'), axis=0, tiled=True)]
    ppermute x0 -> x18, starting transfers between devices: none -> 16.5 us  [the longest x1 3.6 us: exchanged_body(): far_own = lax.ppermute(own, 'branch', far)]
    ppermute x0 -> x18, waiting for transfers between devices: none -> 16.1 us  [the longest x1 5.37 us: exchanged_body(): lax.ppermute(jnp.where(at_end, side, far_side), 'branch', cross)]
    pallas_call x1 -> x4, Pallas kernels: 17.9 us -> 25.2 us  [attend(): pl.pallas_call(functools.partial(attend_kernel, tuple(described), state i...]
    unnamed x0 -> x8, local copies, waits for them, and re-layouts: none -> 3.13 us
    unnamed x2 -> x0, waiting for transfers between devices: 1.41 us -> none
    select_n x0 -> x3, other arithmetic: none -> 1.13 us  [the longest x1 0.98 us: exchanged_body(): cross_own = lax.ppermute(jnp.where(at_end, own, far_own), 'branch', cross)]
  transfers between devices with their start and end apart: 2 -> 18, of which waited for: 2 -> 5; matrix products, arithmetic and copies ran while one was open for 2% -> 5% of each run, Pallas kernels for 0% -> 32%
where the time goes in v2:
time: 65.8 us; the launch traced here: 65.5 us
  Pallas kernels  25.2 us (38%)
  starting transfers between devices  16.5 us (25%)
  waiting for transfers between devices  16.1 us (24%)
  local copies, waits for them, and re-layouts  4.45 us (7%)
  other arithmetic  1.89 us (3%)
  between operations  1.42 us (2%)
    pallas_call x4, Pallas kernels, attend(): pl.pallas_call(functools.partial(attend_kernel, tuple(described), state i...  25.2 us
    ppermute x1, waiting for transfers between devices, exchanged_body(): lax.ppermute(jnp.where(at_end, side, far_side), 'branch', cross)  5.37 us
    ppermute x1, waiting for transfers between devices, exchanged_body(): side = lax.ppermute(own, 'leaf', across)  4.63 us
    ppermute x1, waiting for transfers between devices, exchanged_body(): far_own = lax.ppermute(own, 'branch', far)  4.24 us
    ppermute x1, starting transfers between devices, exchanged_body(): far_own = lax.ppermute(own, 'branch', far)  3.6 us
    unnamed x8, local copies, waits for them, and re-layouts  3.13 us
    ppermute x1, starting transfers between devices, exchanged_body(): cross_own = lax.ppermute(jnp.where(at_end, own, far_own), 'branch', cross)  3.12 us
    ppermute x1, starting transfers between devices, exchanged_body(): branch_side = lax.ppermute(branch_kv, 'leaf', across)  2.97 us
  transfers between devices with their start and end apart: 18, of which 5 were waited for; matrix products, arithmetic and copies ran while one was open for 5% of the time, Pallas kernels for 32%

profile of v2, /device:TPU:0, one launch (start us, length us, event | category | flops | bytes accessed | tf_op | source)
XLA Modules:
  0.0 65.5 jit_solution(8685709933779424798)
XLA Ops:
  0.0 3.0 %collective-permute-start.14 = (bf16[256,1024]{1,0:T(8,128)(2,1)}, bf16[256,1024]{1,0:T(8,128)(2,1)S(1)}, u32[]{:S(2)}, u32[]{:S(2)}) collective-permute-start(bf16[256,1024]{1,0:T(8,128)(2,1)} %param.9), channel_id=1, source_target_pairs={{0,2},{1,3},{2,0},{3,1},{4,6},{5,7},{6,4},{7,5},{8,10},{9,11},{10,... | collective-permute-start | bytes 1572872 | tf_op jit(solution)/shard_map/ppermute | solution.py:170
  3.0 3.6 %collective-permute-start.1 = (bf16[128,1024]{1,0:T(8,128)(2,1)}, bf16[128,1024]{1,0:T(8,128)(2,1)S(1)}, u32[]{:S(2)}, u32[]{:S(2)}) collective-permute-start(bf16[128,1024]{1,0:T(8,128)(2,1)} %refs_3_.1), channel_id=1, source_target_pairs={{0,12},{4,8},{8,4},{12,0},{1,13},{5,9},{9,5},{13,1},{2,14},{6,10},... | collective-permute-start | bytes 786440 | tf_op jit(solution)/shard_map/ppermute | solution.py:167
  6.8 0.5 collective-permute-start
  8.6 1.3 %dynamic_slice.3 = s32[1]{0:T(128)} dynamic-slice(s32[8]{0:T(128)} %param.11, s32[]{:T(128)S(6)} %select_n.48), dynamic_slice_sizes={1} | dynamic-slice | bytes 12 | tf_op jit(solution)/shard_map/dynamic_slice | solution.py:164
  10.0 4.2 %collective-permute-done.1.refs_8_.refs_9_ = bf16[128,1024]{1,0:T(8,128)(2,1)S(1)} collective-permute-done((bf16[128,1024]{1,0:T(8,128)(2,1)}, bf16[128,1024]{1,0:T(8,128)(2,1)S(1)}, u32[]{:S(2)}, u32[]{:S(2)}) %collective-permute-start.1) | collective-permute-done | bytes 262176 | tf_op jit(solution)/shard_map/ppermute | solution.py:167
  14.2 0.3 collective-permute-start.2
  14.5 0.8 %pad_add_fusion.table = s32[3]{0:T(128)S(1)} fusion(s32[1]{0:T(128)S(6)} %copy.8, s32[1]{0:T(128)} %dynamic_slice.3, s32[1]{0:T(128)} %constant.29.clone.1), kind=kLoop, calls=%fused_computation.6 | loop fusion | flops 6 | bytes 24 | tf_op jit(solution)/shard_map/stack | solution.py:164
  15.3 0.7 %collective-permute-done.14 = bf16[256,1024]{1,0:T(8,128)(2,1)S(1)} collective-permute-done((bf16[256,1024]{1,0:T(8,128)(2,1)}, bf16[256,1024]{1,0:T(8,128)(2,1)S(1)}, u32[]{:S(2)}, u32[]{:S(2)}) %collective-permute-start.14) | collective-permute-done | bytes 524320 | tf_op jit(solution)/shard_map/ppermute | solution.py:170
  16.0 1.0 %broadcast_select_fusion.4 = bf16[128,1024]{1,0:T(8,128)(2,1)S(1)} fusion(bf16[128,1024]{1,0:T(8,128)(2,1)} %refs_3_.1, bf16[128,1024]{1,0:T(8,128)(2,1)S(1)} %collective-permute-done.1.refs_8_.refs_9_, pred[]{:T(512)S(6)} %or.3), kind=kLoop, calls=%fused_computation.4 | loop fusion | flops 131072 | bytes 786433 | tf_op jit(solution)/shard_map/jit(_where)/select_n | solution.py:175
  16.9 4.6 %collective-permute-done.refs_0_.refs_1_ = bf16[128,1024]{1,0:T(8,128)(2,1)S(1)} collective-permute-done((bf16[128,1024]{1,0:T(8,128)(2,1)}, bf16[128,1024]{1,0:T(8,128)(2,1)S(1)}, u32[]{:S(2)}, u32[]{:S(2)}) %collective-permute-start) | collective-permute-done | bytes 262176 | tf_op jit(solution)/shard_map/ppermute | solution.py:169
  21.6 3.1 %collective-permute-start.8 = (bf16[128,1024]{1,0:T(8,128)(2,1)S(1)}, bf16[128,1024]{1,0:T(8,128)(2,1)S(1)}, u32[]{:S(2)}, u32[]{:S(2)}) collective-permute-start(bf16[128,1024]{1,0:T(8,128)(2,1)S(1)} %broadcast_select_fusion.4), channel_id=1, source_target_pairs={{4,0},{8,12},{12,4},{0,8},{5,1},{9,13},{13,5},{1,9},{6,2},{10,14},... | collective-permute-start | bytes 786440 | tf_op jit(solution)/shard_map/ppermute | solution.py:175
  24.7 0.5 collective-permute-start.10
  25.2 1.1 %collective-permute-done.2.refs_4_.refs_5_ = bf16[128,1024]{1,0:T(8,128)(2,1)S(1)} collective-permute-done((bf16[128,1024]{1,0:T(8,128)(2,1)S(1)}, bf16[128,1024]{1,0:T(8,128)(2,1)S(1)}, u32[]{:S(2)}, u32[]{:S(2)}) %collective-permute-start.2) | collective-permute-done | bytes 262176 | tf_op jit(solution)/shard_map/ppermute | solution.py:177
  26.3 1.8 %collective-permute-start.5 = (bf16[128,1024]{1,0:T(8,128)(2,1)S(1)}, bf16[128,1024]{1,0:T(8,128)(2,1)S(1)}, u32[]{:S(2)}, u32[]{:S(2)}) collective-permute-start(bf16[128,1024]{1,0:T(8,128)(2,1)S(1)} %collective-permute-done.refs_0_.refs_1_), channel_id=1, source_target_pairs={{0,4},{4,0},{8,12},{12,8},{1,5},{5,1},{9,13},{13,9},{2,6},{6,2},{1... | collective-permute-start | bytes 786440 | tf_op jit(solution)/shard_map/ppermute | solution.py:176
  28.2 1.2 %copy-done = bf16[128,4096]{1,0:T(8,128)(2,1)S(1)} copy-done((bf16[128,4096]{1,0:T(8,128)(2,1)S(1)}, bf16[128,4096]{1,0:T(8,128)(2,1)}, u32[]{:S(2)}) %copy-start) | copy-done | bytes 1048600
  29.4 0.9 %copy-done.1 = bf16[128,1024]{1,0:T(8,128)(2,1)S(1)} copy-done((bf16[128,1024]{1,0:T(8,128)(2,1)S(1)}, bf16[128,1024]{1,0:T(8,128)(2,1)}, u32[]{:S(2)}) %copy-start.1) | copy-done | bytes 262168
  30.3 0.9 %copy-done.2 = bf16[128,1024]{1,0:T(8,128)(2,1)S(1)} copy-done((bf16[128,1024]{1,0:T(8,128)(2,1)S(1)}, bf16[128,1024]{1,0:T(8,128)(2,1)}, u32[]{:S(2)}) %copy-start.2) | copy-done | bytes 262168
  31.3 4.9 %shard_map.73 = (f32[4096,128]{1,0:T(8,128)S(1)}, f32[4096,128]{1,0:T(8,128)S(1)}) custom-call(s32[3]{0:T(128)S(1)} %pad_add_fusion.table, bf16[128,4096]{1,0:T(8,128)(2,1)S(1)} %copy-done, bf16[128,1024]{1,0:T(8,128)(2,1)S(1)} %copy-done.2, bf16[128,1024]{1,0:T(8,128)(2,1)S(1)} %copy-done.2, bf16[128,1024]{1,0:T(8,128)(2,1)S(1)} %copy-done.1, ...), custom_call_target="tpu_custom_call" | custom-call | flops 805306368 | bytes 4194304 | tf_op jit(solution)/shard_map/pallas_call | solution.py:123
  36.3 2.6 %collective-permute-start.3 = (bf16[128,1024]{1,0:T(8,128)(2,1)S(1)}, bf16[128,1024]{1,0:T(8,128)(2,1)S(1)}, u32[]{:S(2)}, u32[]{:S(2)}) collective-permute-start(bf16[128,1024]{1,0:T(8,128)(2,1)S(1)} %broadcast_select_fusion.5), channel_id=1, source_target_pairs={{4,0},{8,12},{12,4},{0,8},{5,1},{9,13},{13,5},{1,9},{6,2},{10,14},... | collective-permute-start | bytes 786440 | tf_op jit(solution)/shard_map/ppermute | solution.py:193
  39.1 0.4 collective-permute-start.9
  39.8 5.4 %collective-permute-done.3.refs_0_.refs_1_ = bf16[128,1024]{1,0:T(8,128)(2,1)S(1)} collective-permute-done((bf16[128,1024]{1,0:T(8,128)(2,1)S(1)}, bf16[128,1024]{1,0:T(8,128)(2,1)S(1)}, u32[]{:S(2)}, u32[]{:S(2)}) %collective-permute-start.3) | collective-permute-done | bytes 262176 | tf_op jit(solution)/shard_map/ppermute | solution.py:193
  45.1 9.5 %shard_map.74 = (f32[4096,128]{1,0:T(8,128)S(1)}, f32[4096,128]{1,0:T(8,128)S(1)}) custom-call(s32[3]{0:T(128)S(1)} %pad_add_fusion.table, bf16[128,4096]{1,0:T(8,128)(2,1)S(1)} %copy-done, bf16[128,1024]{1,0:T(8,128)(2,1)S(1)} %collective-permute-done.refs_0_.refs_1_, bf16[128,1024]{1,0:T(8,128)(2,1)S(1)} %collective-permute-done.refs_0_.refs_1_, ...), custom_call_target="tpu_custom_call" | custom-call | flops 2684354560 | bytes 4194304 | tf_op jit(solution)/shard_map/pallas_call | solution.py:123
  54.7 6.5 %shard_map.75 = (f32[4096,128]{1,0:T(8,128)S(1)}, f32[4096,128]{1,0:T(8,128)S(1)}) custom-call(s32[3]{0:T(128)S(1)} %pad_add_fusion.table, bf16[128,4096]{1,0:T(8,128)(2,1)S(1)} %copy-done, bf16[128,1024]{1,0:T(8,128)(2,1)S(1)} %collective-permute-done.5.refs_0_.refs_1_, bf16[128,1024]{1,0:T(8,128)(2,1)S(1)} %collective-permute-done.5.refs_0_.refs_1_, ...), custom_call_target="tpu_custom_call" | custom-call | flops 1610612736 | bytes 4194304 | tf_op jit(solution)/shard_map/pallas_call | solution.py:123
  61.3 4.3 %shard_map.76 = bf16[128,4096]{1,0:T(8,128)(2,1)} custom-call(s32[3]{0:T(128)S(1)} %pad_add_fusion.table, bf16[128,4096]{1,0:T(8,128)(2,1)S(1)} %copy-done, bf16[128,1024]{1,0:T(8,128)(2,1)S(1)} %collective-permute-done.3.refs_0_.refs_1_, bf16[128,1024]{1,0:T(8,128)(2,1)S(1)} %collective-permute-done.3.refs_0_.refs_1_, ...), custom_call_target="tpu_custom_call" | custom-call | flops 536870912 | bytes 4194304 | tf_op jit(solution)/shard_map/pallas_call | solution.py:123
  (29 shorter events, 0.8 us)
Async XLA Ops:
  0.0 15.9 %collective-permute-start.14 = (bf16[256,1024]{1,0:T(8,128)(2,1)}, bf16[256,1024]{1,0:T(8,128)(2,1)S(1)}, u32[]{:S(2)}, u32[]{:S(2)}) collective-permute-start(bf16[256,1024]{1,0:T(8,128)(2,1)} %param.9), channel_id=1, source_target_pairs={{0,2},{1,3},{2,0},{3,1},{4,6},{5,7},{6,4},{7,5},{8,10},{9,11},{10,... | collective-permute-start | bytes 1572872 | tf_op jit(solution)/shard_map/ppermute | solution.py:170
  3.0 7.0 %collective-permute-start.17 = (bf16[128,1024]{1,0:T(8,128)(2,1)}, bf16[128,1024]{1,0:T(8,128)(2,1)S(1)}, u32[]{:S(2)}, u32[]{:S(2)}) collective-permute-start(bf16[128,1024]{1,0:T(8,128)(2,1)} %refs_3_.1), channel_id=1, source_target_pairs={{0,1},{1,0},{2,3},{3,2},{4,5},{5,4},{6,7},{7,6},{8,9},{9,8},{10,11... | collective-permute-start | bytes 786440 | tf_op jit(solution)/shard_map/ppermute | solution.py:156
  3.0 11.2 %collective-permute-start.1 = (bf16[128,1024]{1,0:T(8,128)(2,1)}, bf16[128,1024]{1,0:T(8,128)(2,1)S(1)}, u32[]{:S(2)}, u32[]{:S(2)}) collective-permute-start(bf16[128,1024]{1,0:T(8,128)(2,1)} %refs_3_.1), channel_id=1, source_target_pairs={{0,12},{4,8},{8,4},{12,0},{1,13},{5,9},{9,5},{13,1},{2,14},{6,10},... | collective-permute-start | bytes 786440 | tf_op jit(solution)/shard_map/ppermute | solution.py:167
  6.6 18.1 %collective-permute-start.16 = (bf16[256,1024]{1,0:T(8,128)(2,1)}, bf16[256,1024]{1,0:T(8,128)(2,1)S(1)}, u32[]{:S(2)}, u32[]{:S(2)}) collective-permute-start(bf16[256,1024]{1,0:T(8,128)(2,1)} %param.9), channel_id=1, source_target_pairs={{0,1},{1,0},{2,3},{3,2},{4,5},{5,4},{6,7},{7,6},{8,9},{9,8},{10,11... | collective-permute-start | bytes 1572872 | tf_op jit(solution)/shard_map/ppermute | solution.py:156
  6.8 14.8 %collective-permute-start = (bf16[128,1024]{1,0:T(8,128)(2,1)}, bf16[128,1024]{1,0:T(8,128)(2,1)S(1)}, u32[]{:S(2)}, u32[]{:S(2)}) collective-permute-start(bf16[128,1024]{1,0:T(8,128)(2,1)} %refs_3_.1), channel_id=1, source_target_pairs={{0,2},{1,3},{2,0},{3,1},{4,6},{5,7},{6,4},{7,5},{8,10},{9,11},{10,... | collective-permute-start | bytes 786440 | tf_op jit(solution)/shard_map/ppermute | solution.py:169
  10.0 14.7 %collective-permute-start.11 = (bf16[128,1024]{1,0:T(8,128)(2,1)}, bf16[128,1024]{1,0:T(8,128)(2,1)S(1)}, u32[]{:S(2)}, u32[]{:S(2)}) collective-permute-start(bf16[128,1024]{1,0:T(8,128)(2,1)} %refs_3_.1), channel_id=1, source_target_pairs={{0,4},{4,0},{8,12},{12,8},{1,5},{5,1},{9,13},{13,9},{2,6},{6,2},{1... | collective-permute-start | bytes 786440 | tf_op jit(solution)/shard_map/ppermute | solution.py:168
  14.2 12.1 %collective-permute-start.2 = (bf16[128,1024]{1,0:T(8,128)(2,1)S(1)}, bf16[128,1024]{1,0:T(8,128)(2,1)S(1)}, u32[]{:S(2)}, u32[]{:S(2)}) collective-permute-start(bf16[128,1024]{1,0:T(8,128)(2,1)S(1)} %collective-permute-done.1.refs_8_.refs_9_), channel_id=1, source_target_pairs={{0,2},{1,3},{2,0},{3,1},{4,6},{5,7},{6,4},{7,5},{8,10},{9,11},{10,... | collective-permute-start | bytes 786440 | tf_op jit(solution)/shard_map/ppermute | solution.py:177
  15.3 24.4 %copy-start.3 = (bf16[256,1024]{1,0:T(8,128)(2,1)S(1)}, bf16[256,1024]{1,0:T(8,128)(2,1)}, u32[]{:S(2)}) copy-start(bf16[256,1024]{1,0:T(8,128)(2,1)} %param.9) | copy-start | bytes 1572868
  15.9 23.5 %collective-permute-start.15 = (bf16[256,1024]{1,0:T(8,128)(2,1)S(1)}, bf16[256,1024]{1,0:T(8,128)(2,1)S(1)}, u32[]{:S(2)}, u32[]{:S(2)}) collective-permute-start(bf16[256,1024]{1,0:T(8,128)(2,1)S(1)} %collective-permute-done.14), channel_id=1, source_target_pairs={{0,1},{1,0},{2,3},{3,2},{4,5},{5,4},{6,7},{7,6},{8,9},{9,8},{10,11... | collective-permute-start | bytes 1572872 | tf_op jit(solution)/shard_map/ppermute | solution.py:156
  21.6 17.4 %collective-permute-start.8 = (bf16[128,1024]{1,0:T(8,128)(2,1)S(1)}, bf16[128,1024]{1,0:T(8,128)(2,1)S(1)}, u32[]{:S(2)}, u32[]{:S(2)}) collective-permute-start(bf16[128,1024]{1,0:T(8,128)(2,1)S(1)} %broadcast_select_fusion.4), channel_id=1, source_target_pairs={{4,0},{8,12},{12,4},{0,8},{5,1},{9,13},{13,5},{1,9},{6,2},{10,14},... | collective-permute-start | bytes 786440 | tf_op jit(solution)/shard_map/ppermute | solution.py:175
  24.7 11.6 %collective-permute-start.13 = (bf16[128,1024]{1,0:T(8,128)(2,1)S(1)}, bf16[128,1024]{1,0:T(8,128)(2,1)S(1)}, u32[]{:S(2)}, u32[]{:S(2)}) collective-permute-start(bf16[128,1024]{1,0:T(8,128)(2,1)S(1)} %collective-permute-done.1.refs_8_.refs_9_), channel_id=1, source_target_pairs={{0,1},{1,0},{2,3},{3,2},{4,5},{5,4},{6,7},{7,6},{8,9},{9,8},{10,11... | collective-permute-start | bytes 786440 | tf_op jit(solution)/shard_map/ppermute | solution.py:156
  24.7 11.5 %collective-permute-start.10 = (bf16[128,1024]{1,0:T(8,128)(2,1)S(1)}, bf16[128,1024]{1,0:T(8,128)(2,1)S(1)}, u32[]{:S(2)}, u32[]{:S(2)}) collective-permute-start(bf16[128,1024]{1,0:T(8,128)(2,1)S(1)} %collective-permute-done.refs_0_.refs_1_), channel_id=1, source_target_pairs={{0,1},{1,0},{2,3},{3,2},{4,5},{5,4},{6,7},{7,6},{8,9},{9,8},{10,11... | collective-permute-start | bytes 786440 | tf_op jit(solution)/shard_map/ppermute | solution.py:156
  26.3 12.8 %collective-permute-start.5 = (bf16[128,1024]{1,0:T(8,128)(2,1)S(1)}, bf16[128,1024]{1,0:T(8,128)(2,1)S(1)}, u32[]{:S(2)}, u32[]{:S(2)}) collective-permute-start(bf16[128,1024]{1,0:T(8,128)(2,1)S(1)} %collective-permute-done.refs_0_.refs_1_), channel_id=1, source_target_pairs={{0,4},{4,0},{8,12},{12,8},{1,5},{5,1},{9,13},{13,9},{2,6},{6,2},{1... | collective-permute-start | bytes 786440 | tf_op jit(solution)/shard_map/ppermute | solution.py:176
  28.2 1.2 %copy-start = (bf16[128,4096]{1,0:T(8,128)(2,1)S(1)}, bf16[128,4096]{1,0:T(8,128)(2,1)}, u32[]{:S(2)}) copy-start(bf16[128,4096]{1,0:T(8,128)(2,1)} %query_ref.7) | copy-start | bytes 3145732
  29.4 0.9 %copy-start.1 = (bf16[128,1024]{1,0:T(8,128)(2,1)S(1)}, bf16[128,1024]{1,0:T(8,128)(2,1)}, u32[]{:S(2)}) copy-start(bf16[128,1024]{1,0:T(8,128)(2,1)} %refs_3_.1) | copy-start | bytes 786436
  30.3 0.9 %copy-start.2 = (bf16[128,1024]{1,0:T(8,128)(2,1)S(1)}, bf16[128,1024]{1,0:T(8,128)(2,1)}, u32[]{:S(2)}) copy-start(bf16[128,1024]{1,0:T(8,128)(2,1)} %refs_1_.1) | copy-start | bytes 786436
  36.2 8.9 %collective-permute-start.12 = (bf16[128,1024]{1,0:T(8,128)(2,1)S(1)}, bf16[128,1024]{1,0:T(8,128)(2,1)S(1)}, u32[]{:S(2)}, u32[]{:S(2)}) collective-permute-start(bf16[128,1024]{1,0:T(8,128)(2,1)S(1)} %collective-permute-done.11.refs_4_.refs_5_), channel_id=1, source_target_pairs={{0,1},{1,0},{2,3},{3,2},{4,5},{5,4},{6,7},{7,6},{8,9},{9,8},{10,11... | collective-permute-start | bytes 786440 | tf_op jit(solution)/shard_map/ppermute | solution.py:156
  36.3 8.8 %collective-permute-start.3 = (bf16[128,1024]{1,0:T(8,128)(2,1)S(1)}, bf16[128,1024]{1,0:T(8,128)(2,1)S(1)}, u32[]{:S(2)}, u32[]{:S(2)}) collective-permute-start(bf16[128,1024]{1,0:T(8,128)(2,1)S(1)} %broadcast_select_fusion.5), channel_id=1, source_target_pairs={{4,0},{8,12},{12,4},{0,8},{5,1},{9,13},{13,5},{1,9},{6,2},{10,14},... | collective-permute-start | bytes 786440 | tf_op jit(solution)/shard_map/ppermute | solution.py:193
  39.0 15.7 %collective-permute-start.7 = (bf16[128,1024]{1,0:T(8,128)(2,1)S(1)}, bf16[128,1024]{1,0:T(8,128)(2,1)S(1)}, u32[]{:S(2)}, u32[]{:S(2)}) collective-permute-start(bf16[128,1024]{1,0:T(8,128)(2,1)S(1)} %collective-permute-done.2.refs_4_.refs_5_), channel_id=1, source_target_pairs={{0,1},{1,0},{2,3},{3,2},{4,5},{5,4},{6,7},{7,6},{8,9},{9,8},{10,11... | collective-permute-start | bytes 786440 | tf_op jit(solution)/shard_map/ppermute | solution.py:156
  39.1 15.6 %collective-permute-start.9 = (bf16[128,1024]{1,0:T(8,128)(2,1)S(1)}, bf16[128,1024]{1,0:T(8,128)(2,1)S(1)}, u32[]{:S(2)}, u32[]{:S(2)}) collective-permute-start(bf16[128,1024]{1,0:T(8,128)(2,1)S(1)} %collective-permute-done.8.refs_8_.refs_9_), channel_id=1, source_target_pairs={{0,1},{1,0},{2,3},{3,2},{4,5},{5,4},{6,7},{7,6},{8,9},{9,8},{10,11... | collective-permute-start | bytes 786440 | tf_op jit(solution)/shard_map/ppermute | solution.py:156
  39.5 15.2 %collective-permute-start.6 = (bf16[128,1024]{1,0:T(8,128)(2,1)S(1)}, bf16[128,1024]{1,0:T(8,128)(2,1)S(1)}, u32[]{:S(2)}, u32[]{:S(2)}) collective-permute-start(bf16[128,1024]{1,0:T(8,128)(2,1)S(1)} %collective-permute-done.5.refs_0_.refs_1_), channel_id=1, source_target_pairs={{0,1},{1,0},{2,3},{3,2},{4,5},{5,4},{6,7},{7,6},{8,9},{9,8},{10,11... | collective-permute-start | bytes 786440 | tf_op jit(solution)/shard_map/ppermute | solution.py:156
  45.1 16.1 %collective-permute-start.4 = (bf16[128,1024]{1,0:T(8,128)(2,1)S(1)}, bf16[128,1024]{1,0:T(8,128)(2,1)S(1)}, u32[]{:S(2)}, u32[]{:S(2)}) collective-permute-start(bf16[128,1024]{1,0:T(8,128)(2,1)S(1)} %collective-permute-done.3.refs_0_.refs_1_), channel_id=1, source_target_pairs={{0,1},{1,0},{2,3},{3,2},{4,5},{5,4},{6,7},{7,6},{8,9},{9,8},{10,11... | collective-permute-start | bytes 786440 | tf_op jit(solution)/shard_map/ppermute | solution.py:156

commit v3 on v1

v3 whole, which is shorter than its diff:
```python
import functools
import math

import jax
import jax.numpy as jnp
from jax import lax
from jax.experimental import pallas as pl
from jax.experimental.pallas import tpu as pltpu
from jax.sharding import PartitionSpec as P


QH = 32
KVH = 4
DH = 128
BR_DEV = 2
BL = 512


neg_large = -1e30
key_tile = 256
kernel_vmem = 28 * 1024 * 1024
vmem = pl.BlockSpec(memory_space=pltpu.VMEM)
smem = pl.BlockSpec(memory_space=pltpu.SMEM)
anywhere = pl.BlockSpec(memory_space=pl.ANY)


def tiles_of(spans, scalars):
    tiles = []
    for kind, refs in spans:
        if kind == "root":
            pending, height = [], 0
            for ref in refs:
                for start in range(0, ref.shape[0], key_tile):
                    size = min(key_tile, ref.shape[0] - start)
                    pending.append((ref, start, size))
                    height += size
                    if height >= key_tile:
                        tiles.append((pending, height, None, None))
                        pending, height = [], 0
            if pending:
                tiles.append((pending, height, None, None))
        elif kind == "leaf":
            tiles.append(([(refs[0], 0, refs[0].shape[0])], refs[0].shape[0], "leaf", 0))
        elif kind == "trunk":
            base = scalars["local_branch"] * BL
            for start in range(0, BL, key_tile):
                tiles.append(([(refs[0], base + start, key_tile)], key_tile, "branch", start))
        else:
            half = refs[0].shape[0]
            first = scalars["core"] * half
            tiles.append(([refs[0:2]], half, "branch", first))
            tiles.append(([refs[2:4]], half, "branch", half - first))
    return tiles


def load(parts, lanes, scalars):
    pieces = []
    for part in parts:
        if len(part) == 2:
            near, far = part
            pieces.append(jnp.where(scalars["elsewhere"], far[:, lanes], near[:, lanes]))
        else:
            ref, start, size = part
            if not isinstance(start, int):
                start = pl.multiple_of(start, key_tile)
            pieces.append(ref[pl.ds(start, size), lanes])
    return pieces[0] if len(pieces) == 1 else jnp.concatenate(pieces, axis=0)


def attend_kernel(kinds, carries, finishes, *refs):
    refs = list(refs)
    scalars = {}
    if any(kind in ("trunk", "branch") for kind, count in kinds):
        parent_ref, length_ref = refs.pop(0), refs.pop(0)
        parent = parent_ref[0]
        place = lax.axis_index("leaf")
        local_branch = parent - lax.axis_index("branch") * BR_DEV
        scalars = dict(
            local_branch=local_branch,
            length=length_ref[parent],
            core=lax.rem(place, 2),
            elsewhere=local_branch != lax.div(place, 2),
        )
    live_ref = refs.pop(0) if finishes else None
    query_ref = refs.pop(0)
    spans = [(kind, [refs.pop(0) for _ in range(count)]) for kind, count in kinds]
    if carries:
        old_total, old_max = refs.pop(0), refs.pop(0)
    tiles = tiles_of(spans, scalars)
    row_count = query_ref.shape[0]
    groups = query_ref.shape[1] // (DH * KVH)
    total_rows = row_count * groups
    factor = DH ** -0.5 * math.log2(math.e)

    def head(k, unused):
        def lanes_at(number):
            return pl.ds(pl.multiple_of(number * DH, DH), DH)

        rows = pl.ds(pl.multiple_of(k * total_rows, total_rows), total_rows)
        query = jnp.concatenate([query_ref[:, lanes_at(k * groups + g)] for g in range(groups)], axis=0)
        if carries:
            total = jnp.concatenate([old_total[rows, :], jnp.ones((total_rows, DH), jnp.float32)], axis=1)
            row_max = jnp.max(old_max[rows, :], axis=1, keepdims=True)
        else:
            row_max = jnp.full((total_rows, 1), neg_large, jnp.float32)
            total = None
        for parts, size, mask, offset in tiles:
            keys = load(parts, lanes_at(k), scalars)
            values = load(parts, lanes_at(KVH + k), scalars)
            scores = lax.dot_general(
                query, keys, (((1,), (1,)), ((), ())), preferred_element_type=jnp.float32
            )
            if mask is not None:
                column = lax.broadcasted_iota(jnp.int32, scores.shape, 1)
                if mask == "leaf":
                    row = lax.rem(lax.broadcasted_iota(jnp.int32, scores.shape, 0), row_count)
                    visible = column <= row
                else:
                    visible = column < scalars["length"] - offset
                scores = jnp.where(visible, scores, neg_large)
            new_max = jnp.maximum(row_max, jnp.max(scores, axis=1, keepdims=True))
            weights = jnp.exp2((scores - new_max) * factor).astype(jnp.bfloat16)
            padded = jnp.concatenate([values, jnp.ones_like(values)], axis=1)
            product = jnp.dot(weights, padded, preferred_element_type=jnp.float32)
            if total is None:
                total = product
            else:
                total = total * jnp.exp2((row_max - new_max) * factor) + product
            row_max = new_max
        result = total[:, :DH] / total[:, DH:]
        if finishes:
            out_ref, held_ref, sems = refs
            live = lax.broadcasted_iota(jnp.int32, (row_count, DH), 0) < live_ref[0]
            for g in range(groups):
                piece = result[g * row_count:(g + 1) * row_count]
                held_ref[k, :, g * DH:(g + 1) * DH] = jnp.where(live, piece, 0.0).astype(held_ref.dtype)
            pltpu.make_async_copy(held_ref.at[k], out_of(out_ref, k), sems.at[k]).start()
        else:
            refs[0][rows, :] = result
            refs[1][rows, :] = row_max + jnp.log2(total[:, DH:]) * (1.0 / factor)
        return unused

    def out_of(out_ref, k):
        width = groups * DH
        return out_ref.at[:, pl.ds(pl.multiple_of(k * width, width), width)]

    lax.fori_loop(0, KVH, head, 0)
    if finishes:
        out_ref, held_ref, sems = refs
        for k in range(KVH):
            pltpu.make_async_copy(held_ref.at[k], out_of(out_ref, k), sems.at[k]).wait()


def attend(numbers, queries, spans, state=None, finishes=False):
    row_count = queries.shape[0]
    groups = QH // KVH
    parent, branch_len, leaf_len = numbers
    operands, in_specs = [], []
    if any(kind in ("trunk", "branch") for kind, arrays in spans):
        operands += [parent, branch_len]
        in_specs += [smem, smem]
    if finishes:
        operands.append(leaf_len)
        in_specs.append(smem)
    arrays = [queries] + [array for kind, listed in spans for array in listed]
    operands += arrays
    in_specs += [vmem] * len(arrays)
    aliases = {}
    if state is not None:
        if not finishes:
            aliases = {len(operands): 0, len(operands) + 1: 1}
        operands += state
        in_specs += [vmem, vmem]
    scratch = ()
    if finishes:
        out_specs = anywhere
        out_shape = jax.ShapeDtypeStruct(queries.shape, queries.dtype)
        scratch = (
            pltpu.VMEM((KVH, row_count, groups * DH), queries.dtype),
            pltpu.SemaphoreType.DMA((KVH,)),
        )
    else:
        part = jax.ShapeDtypeStruct((KVH * row_count * groups, DH), jnp.float32)
        out_specs, out_shape = [vmem, vmem], [part, part]
    key_count = sum(array.shape[0] for kind, listed in spans for array in listed)
    return pl.pallas_call(
        functools.partial(
            attend_kernel, tuple((kind, len(listed)) for kind, listed in spans), state is not None, finishes
        ),
        in_specs=in_specs,
        out_specs=out_specs,
        out_shape=out_shape,
        scratch_shapes=scratch,
        input_output_aliases=aliases,
        compiler_params=pltpu.CompilerParams(vmem_limit_bytes=kernel_vmem),
        cost_estimate=pl.CostEstimate(
            flops=4 * row_count * QH * DH * key_count,
            bytes_accessed=2 * row_count * QH * DH * 4,
            transcendentals=row_count * QH * key_count,
        ),
    )(*operands)


def pick_kernel(end_ref, middle_ref, out_ref):
    z = lax.axis_index("branch")
    at_end = (z == 0) | (z == lax.axis_size("branch") - 1)

    @pl.when(at_end)
    def _():
        out_ref[...] = end_ref[...]

    @pl.when(jnp.logical_not(at_end))
    def _():
        out_ref[...] = middle_ref[...]


def pick(end_rows, middle_rows):
    return pl.pallas_call(
        pick_kernel,
        in_specs=[vmem, vmem],
        out_specs=vmem,
        out_shape=jax.ShapeDtypeStruct(end_rows.shape, end_rows.dtype),
        compiler_params=pltpu.CompilerParams(vmem_limit_bytes=4 * 1024 * 1024),
    )(end_rows, middle_rows)


def gathered_body(queries, leaf_kv, branch_kv, root_kv, branch_len, leaf_len, leaf_parent):
    trunk_rows = lax.all_gather(branch_kv, "leaf", axis=0, tiled=True)
    whole_root = lax.all_gather(root_kv, ("branch", "leaf"), axis=0, tiled=True)
    numbers = (leaf_parent, branch_len, leaf_len)
    spans = [("leaf", [leaf_kv]), ("trunk", [trunk_rows]), ("root", [whole_root])]
    return attend(numbers, queries, spans, finishes=True)


def exchanged_body(queries, leaf_kv, branch_kv, root_kv, branch_len, leaf_len, leaf_parent):
    across = [(i, i ^ 2) for i in range(4)]
    beside = [(i, i ^ 1) for i in range(4)]
    near = [(i, i ^ 1) for i in range(4)]
    far = [(i, i ^ 3) for i in range(4)]
    cross = [(1, 0), (2, 3), (3, 1), (0, 2)]
    numbers = (leaf_parent, branch_len, leaf_len)

    def swap(rows):
        return lax.ppermute(rows, "leaf", beside)

    own = root_kv
    far_own = lax.ppermute(own, "branch", far)
    near_own = lax.ppermute(own, "branch", near)
    side = lax.ppermute(own, "leaf", across)
    branch_side = lax.ppermute(branch_kv, "leaf", across)
    own_swapped = swap(own)
    branch_swapped = swap(branch_kv)
    state = attend(numbers, queries, [("leaf", [leaf_kv]), ("root", [own, own_swapped])])

    cross_own = lax.ppermute(pick(own, far_own), "branch", cross)
    near_side = lax.ppermute(side, "branch", near)
    far_side = lax.ppermute(far_own, "leaf", across)
    side_swapped = swap(side)
    near_own_swapped = swap(near_own)
    far_own_swapped = swap(far_own)
    branch_side_swapped = swap(branch_side)
    state = attend(numbers, queries, [
        ("root", [side, near_own, far_own, side_swapped, near_own_swapped, far_own_swapped]),
    ], state)

    cross_side = lax.ppermute(pick(side, far_side), "branch", cross)
    near_side_swapped = swap(near_side)
    far_side_swapped = swap(far_side)
    cross_own_swapped = swap(cross_own)
    state = attend(numbers, queries, [("branch", [branch_kv, branch_side, branch_swapped, branch_side_swapped])], state)
    state = attend(numbers, queries, [
        ("root", [near_side, far_side, cross_own, near_side_swapped, far_side_swapped, cross_own_swapped]),
    ], state)
    cross_side_swapped = swap(cross_side)
    return attend(numbers, queries, [("root", [cross_side, cross_side_swapped])], state, finishes=True)


def solution(mesh):
    split = P(("rep", "branch", "leaf"), None)
    single = P(("rep", "branch", "leaf"))
    small = mesh.shape["branch"] == 4 and mesh.shape["leaf"] == 4
    return jax.shard_map(
        exchanged_body if small else gathered_body,
        mesh=mesh,
        in_specs=(split, split, split, split, P("rep"), single, single),
        out_specs=split,
        check_vma=False,
    )
```

time: 112 us -> 59.7 us (0.53)
  waiting for transfers between devices: 76.3 us -> 13.1 us
  starting transfers between devices: 0.04 us -> 17.9 us
  between operations: 14.7 us -> 1.46 us
  Pallas kernels: 17.9 us -> 22.9 us
  local copies, waits for them, and re-layouts: 1.24 us -> 4.08 us
  other arithmetic: 1.29 us -> 0 us
    all_gather x2 -> x0, waiting for transfers between devices: 74.9 us -> none  [the longest x1 52.6 us: body(): whole_root = lax.all_gather(root_kv, ('branch', 'leaf'), axis=0, tiled=True)]
    ppermute x0 -> x18, starting transfers between devices: none -> 17.9 us  [the longest x1 4.07 us: exchanged_body(): far_own = lax.ppermute(own, 'branch', far)]
    ppermute x0 -> x18, waiting for transfers between devices: none -> 13.1 us  [the longest x1 4.14 us: exchanged_body(): far_own = lax.ppermute(own, 'branch', far)]
    pallas_call x1 -> x7, Pallas kernels: 17.9 us -> 22.9 us  [the longest x5 22.9 us: attend(): pl.pallas_call(functools.partial(attend_kernel, tuple(((kind, len(listed)...]
    unnamed x0 -> x14, local copies, waits for them, and re-layouts: none -> 4.08 us
    unnamed x2 -> x0, waiting for transfers between devices: 1.41 us -> none
    another operation x1 -> x0, other arithmetic: 1.29 us -> none  [body(): table = jnp.stack([local_branch, branch_len[parent], leaf_len[0]])]
    dynamic_slice x1 -> x0, local copies, waits for them, and re-layouts: 1.24 us -> none  [body(): table = jnp.stack([local_branch, branch_len[parent], leaf_len[0]])]
  transfers between devices with their start and end apart: 2 -> 18, of which waited for: 2 -> 5; matrix products, arithmetic and copies ran while one was open for 2% -> 0% of each run, Pallas kernels for 0% -> 33%
where the time goes in v3:
time: 59.7 us; the launch traced here: 59.4 us
  Pallas kernels  22.9 us (38%)
  starting transfers between devices  17.9 us (30%)
  waiting for transfers between devices  13.1 us (22%)
  local copies, waits for them, and re-layouts  4.08 us (7%)
  between operations  1.46 us (2%)
    pallas_call x5, Pallas kernels, attend(): pl.pallas_call(functools.partial(attend_kernel, tuple(((kind, len(listed)...  22.9 us
    ppermute x1, waiting for transfers between devices, exchanged_body(): far_own = lax.ppermute(own, 'branch', far)  4.14 us
    unnamed x14, local copies, waits for them, and re-layouts  4.08 us
    ppermute x1, starting transfers between devices, exchanged_body(): far_own = lax.ppermute(own, 'branch', far)  4.07 us
    ppermute x1, waiting for transfers between devices, exchanged_body(): near_own = lax.ppermute(own, 'branch', near)  3.79 us
    ppermute x1, starting transfers between devices, exchanged_body(): cross_own = lax.ppermute(pick(own, far_own), 'branch', cross)  3.79 us
    ppermute x1, waiting for transfers between devices, exchanged_body(): side = lax.ppermute(own, 'leaf', across)  3.22 us
    ppermute x1, starting transfers between devices, exchanged_body(): side = lax.ppermute(own, 'leaf', across)  2.97 us
  transfers between devices with their start and end apart: 18, of which 5 were waited for; matrix products, arithmetic and copies ran while one was open for 0% of the time, Pallas kernels for 33%

profile of v3, /device:TPU:0, one launch (start us, length us, event | category | flops | bytes accessed | tf_op | source)
XLA Modules:
  0.0 59.4 jit_solution(8595689049079560058)
XLA Ops:
  0.0 3.0 %collective-permute-start = (bf16[128,1024]{1,0:T(8,128)(2,1)}, bf16[128,1024]{1,0:T(8,128)(2,1)S(1)}, u32[]{:S(2)}, u32[]{:S(2)}) collective-permute-start(bf16[128,1024]{1,0:T(8,128)(2,1)} %refs_2_.2), channel_id=1, source_target_pairs={{0,2},{1,3},{2,0},{3,1},{4,6},{5,7},{6,4},{7,5},{8,10},{9,11},{10,... | collective-permute-start | bytes 786440 | tf_op jit(solution)/shard_map/ppermute | solution.py:249
  3.0 4.1 %collective-permute-start.1 = (bf16[128,1024]{1,0:T(8,128)(2,1)}, bf16[128,1024]{1,0:T(8,128)(2,1)S(1)}, u32[]{:S(2)}, u32[]{:S(2)}) collective-permute-start(bf16[128,1024]{1,0:T(8,128)(2,1)} %refs_2_.2), channel_id=1, source_target_pairs={{0,12},{4,8},{8,4},{12,0},{1,13},{5,9},{9,5},{13,1},{2,14},{6,10},... | collective-permute-start | bytes 786440 | tf_op jit(solution)/shard_map/ppermute | solution.py:247
  7.1 3.2 %collective-permute-done.end_ref.refs_1_ = bf16[128,1024]{1,0:T(8,128)(2,1)S(1)} collective-permute-done((bf16[128,1024]{1,0:T(8,128)(2,1)}, bf16[128,1024]{1,0:T(8,128)(2,1)S(1)}, u32[]{:S(2)}, u32[]{:S(2)}) %collective-permute-start) | collective-permute-done | bytes 262176 | tf_op jit(solution)/shard_map/ppermute | solution.py:249
  10.3 4.1 %collective-permute-done.1.middle_ref.refs_3_ = bf16[128,1024]{1,0:T(8,128)(2,1)S(1)} collective-permute-done((bf16[128,1024]{1,0:T(8,128)(2,1)}, bf16[128,1024]{1,0:T(8,128)(2,1)S(1)}, u32[]{:S(2)}, u32[]{:S(2)}) %collective-permute-start.1) | collective-permute-done | bytes 262176 | tf_op jit(solution)/shard_map/ppermute | solution.py:247
  14.5 0.5 collective-permute-start.16
  15.0 3.8 %collective-permute-done.13.refs_2_ = bf16[128,1024]{1,0:T(8,128)(2,1)S(1)} collective-permute-done((bf16[128,1024]{1,0:T(8,128)(2,1)}, bf16[128,1024]{1,0:T(8,128)(2,1)S(1)}, u32[]{:S(2)}, u32[]{:S(2)}) %collective-permute-start.13) | collective-permute-done | bytes 262176 | tf_op jit(solution)/shard_map/ppermute | solution.py:248
  18.8 1.5 %collective-permute-start.2 = (bf16[128,1024]{1,0:T(8,128)(2,1)S(1)}, bf16[128,1024]{1,0:T(8,128)(2,1)S(1)}, u32[]{:S(2)}, u32[]{:S(2)}) collective-permute-start(bf16[128,1024]{1,0:T(8,128)(2,1)S(1)} %collective-permute-done.1.middle_ref.refs_3_), channel_id=1, source_target_pairs={{0,2},{1,3},{2,0},{3,1},{4,6},{5,7},{6,4},{7,5},{8,10},{9,11},{10,... | collective-permute-start | bytes 786440 | tf_op jit(solution)/shard_map/ppermute | solution.py:257
  20.3 0.4 collective-permute-done.10.refs_4_
  20.8 0.9 %copy-done.2 = bf16[128,1024]{1,0:T(8,128)(2,1)S(1)} copy-done((bf16[128,1024]{1,0:T(8,128)(2,1)S(1)}, bf16[128,1024]{1,0:T(8,128)(2,1)}, u32[]{:S(2)}) %copy-start.2) | copy-done | bytes 262168
  21.8 3.8 %collective-permute-start.6 = (bf16[128,1024]{1,0:T(8,128)(2,1)S(1)}, bf16[128,1024]{1,0:T(8,128)(2,1)S(1)}, u32[]{:S(2)}, u32[]{:S(2)}) collective-permute-start(bf16[128,1024]{1,0:T(8,128)(2,1)S(1)} %shard_map.74), channel_id=1, source_target_pairs={{4,0},{8,12},{12,4},{0,8},{5,1},{9,13},{13,5},{1,9},{6,2},{10,14},... | collective-permute-start | bytes 786440 | tf_op jit(solution)/shard_map/ppermute | solution.py:255
  25.6 1.5 %collective-permute-done.2.middle_ref.refs_2_ = bf16[128,1024]{1,0:T(8,128)(2,1)S(1)} collective-permute-done((bf16[128,1024]{1,0:T(8,128)(2,1)S(1)}, bf16[128,1024]{1,0:T(8,128)(2,1)S(1)}, u32[]{:S(2)}, u32[]{:S(2)}) %collective-permute-start.2) | collective-permute-done | bytes 262176 | tf_op jit(solution)/shard_map/ppermute | solution.py:257
  27.1 1.1 %collective-permute-start.5 = (bf16[128,1024]{1,0:T(8,128)(2,1)S(1)}, bf16[128,1024]{1,0:T(8,128)(2,1)S(1)}, u32[]{:S(2)}, u32[]{:S(2)}) collective-permute-start(bf16[128,1024]{1,0:T(8,128)(2,1)S(1)} %collective-permute-done.end_ref.refs_1_), channel_id=1, source_target_pairs={{0,4},{4,0},{8,12},{12,8},{1,5},{5,1},{9,13},{13,9},{2,6},{6,2},{1... | collective-permute-start | bytes 786440 | tf_op jit(solution)/shard_map/ppermute | solution.py:256
  28.2 2.6 %collective-permute-start.3 = (bf16[128,1024]{1,0:T(8,128)(2,1)S(1)}, bf16[128,1024]{1,0:T(8,128)(2,1)S(1)}, u32[]{:S(2)}, u32[]{:S(2)}) collective-permute-start(bf16[128,1024]{1,0:T(8,128)(2,1)S(1)} %shard_map.73), channel_id=1, source_target_pairs={{4,0},{8,12},{12,4},{0,8},{5,1},{9,13},{13,5},{1,9},{6,2},{10,14},... | collective-permute-start | bytes 786440 | tf_op jit(solution)/shard_map/ppermute | solution.py:266
  32.2 1.2 %copy-done = bf16[128,4096]{1,0:T(8,128)(2,1)S(1)} copy-done((bf16[128,4096]{1,0:T(8,128)(2,1)S(1)}, bf16[128,4096]{1,0:T(8,128)(2,1)}, u32[]{:S(2)}) %copy-start) | copy-done | bytes 1048600
  33.4 0.9 %copy-done.3 = bf16[128,1024]{1,0:T(8,128)(2,1)S(1)} copy-done((bf16[128,1024]{1,0:T(8,128)(2,1)S(1)}, bf16[128,1024]{1,0:T(8,128)(2,1)}, u32[]{:S(2)}) %copy-start.3) | copy-done | bytes 262168
  34.3 0.9 %copy-done.5 = bf16[128,1024]{1,0:T(8,128)(2,1)S(1)} copy-done((bf16[128,1024]{1,0:T(8,128)(2,1)S(1)}, bf16[128,1024]{1,0:T(8,128)(2,1)}, u32[]{:S(2)}) %copy-start.5) | copy-done | bytes 262168
  35.3 4.0 %shard_map.75 = (f32[4096,128]{1,0:T(8,128)S(1)}, f32[4096,128]{1,0:T(8,128)S(1)}) custom-call(bf16[128,4096]{1,0:T(8,128)(2,1)S(1)} %copy-done, bf16[128,1024]{1,0:T(8,128)(2,1)S(1)} %copy-done.5, bf16[128,1024]{1,0:T(8,128)(2,1)S(1)} %copy-done.3, bf16[128,1024]{1,0:T(8,128)(2,1)S(1)} %collective-permute-done.17.refs_3_), custom_call_target="tpu_custom_call" | custom-call | flops 805306368 | bytes 4194304 | tf_op jit(solution)/shard_map/pallas_call | solution.py:186
  39.3 0.5 collective-permute-start.9
  39.8 0.1 collective-permute-start.7
  39.9 5.4 %shard_map.76 = (f32[4096,128]{1,0:T(8,128)S(1)}, f32[4096,128]{1,0:T(8,128)S(1)}) custom-call(bf16[128,4096]{1,0:T(8,128)(2,1)S(1)} %copy-done.1, bf16[128,1024]{1,0:T(8,128)(2,1)S(1)} %collective-permute-done.end_ref.refs_1_, bf16[128,1024]{1,0:T(8,128)(2,1)S(1)} %collective-permute-done.13.refs_2_, ...), custom_call_target="tpu_custom_call", output_to_operand_aliasing={{0}: (7, {}), {1}: (8, {})} | custom-call | flops 1610612736 | bytes 4194304 | tf_op jit(solution)/shard_map/pallas_call | solution.py:186
  45.4 0.5 collective-permute-start.4
  45.9 4.6 %shard_map.77 = (f32[4096,128]{1,0:T(8,128)S(1)}, f32[4096,128]{1,0:T(8,128)S(1)}) custom-call(s32[1]{0:T(128)S(6)} %copy.21.refs_0_, s32[8]{0:T(128)S(1)} %copy-done.6, bf16[128,4096]{1,0:T(8,128)(2,1)S(1)} %copy-done.1, bf16[256,1024]{1,0:T(8,128)(2,1)S(1)} %copy-done.4, ...), custom_call_target="tpu_custom_call", output_to_operand_aliasing={{0}: (7, {}), {1}: (8, {})} | custom-call | flops 2147483648 | bytes 4194304 | tf_op jit(solution)/shard_map/pallas_call | solution.py:186
  50.5 5.4 %shard_map.78 = (f32[4096,128]{1,0:T(8,128)S(1)}, f32[4096,128]{1,0:T(8,128)S(1)}) custom-call(bf16[128,4096]{1,0:T(8,128)(2,1)S(1)} %copy-done.1, bf16[128,1024]{1,0:T(8,128)(2,1)S(1)} %collective-permute-done.5.refs_1_, bf16[128,1024]{1,0:T(8,128)(2,1)S(1)} %collective-permute-done.2.middle_ref.refs_2_, ...), custom_call_target="tpu_custom_call", output_to_operand_aliasing={{0}: (7, {}), {1}: (8, {})} | custom-call | flops 1610612736 | bytes 4194304 | tf_op jit(solution)/shard_map/pallas_call | solution.py:186
  56.0 3.4 %shard_map.79 = bf16[128,4096]{1,0:T(8,128)(2,1)} custom-call(s32[1]{0:T(128)S(6)} %copy.20.refs_0_, bf16[128,4096]{1,0:T(8,128)(2,1)S(1)} %copy-done.1, bf16[128,1024]{1,0:T(8,128)(2,1)S(1)} %collective-permute-done.3.refs_2_, bf16[128,1024]{1,0:T(8,128)(2,1)S(1)} %collective-permute-done.4.refs_3_, f32[4096,128]{1,0:T(8,128)S(1)} %get-tuple-element.19.refs_4_, ...), custom_call_target="tpu_custom_call" | custom-call | flops 536870912 | bytes 4194304 | tf_op jit(solution)/shard_map/pallas_call | solution.py:186
  (33 shorter events, 0.3 us)
Async XLA Ops:
  0.0 39.9 %copy-start.1 = (bf16[128,4096]{1,0:T(8,128)(2,1)S(1)}, bf16[128,4096]{1,0:T(8,128)(2,1)}, u32[]{:S(2)}) copy-start(bf16[128,4096]{1,0:T(8,128)(2,1)} %refs_1_.5) | copy-start | bytes 3145732
  0.0 10.3 %collective-permute-start = (bf16[128,1024]{1,0:T(8,128)(2,1)}, bf16[128,1024]{1,0:T(8,128)(2,1)S(1)}, u32[]{:S(2)}, u32[]{:S(2)}) collective-permute-start(bf16[128,1024]{1,0:T(8,128)(2,1)} %refs_2_.2), channel_id=1, source_target_pairs={{0,2},{1,3},{2,0},{3,1},{4,6},{5,7},{6,4},{7,5},{8,10},{9,11},{10,... | collective-permute-start | bytes 786440 | tf_op jit(solution)/shard_map/ppermute | solution.py:249
  3.0 17.7 %collective-permute-start.10 = (bf16[256,1024]{1,0:T(8,128)(2,1)}, bf16[256,1024]{1,0:T(8,128)(2,1)S(1)}, u32[]{:S(2)}, u32[]{:S(2)}) collective-permute-start(bf16[256,1024]{1,0:T(8,128)(2,1)} %refs_3_.1), channel_id=1, source_target_pairs={{0,2},{1,3},{2,0},{3,1},{4,6},{5,7},{6,4},{7,5},{8,10},{9,11},{10,... | collective-permute-start | bytes 1572872 | tf_op jit(solution)/shard_map/ppermute | solution.py:250
  3.0 11.4 %collective-permute-start.1 = (bf16[128,1024]{1,0:T(8,128)(2,1)}, bf16[128,1024]{1,0:T(8,128)(2,1)S(1)}, u32[]{:S(2)}, u32[]{:S(2)}) collective-permute-start(bf16[128,1024]{1,0:T(8,128)(2,1)} %refs_2_.2), channel_id=1, source_target_pairs={{0,12},{4,8},{8,4},{12,0},{1,13},{5,9},{9,5},{13,1},{2,14},{6,10},... | collective-permute-start | bytes 786440 | tf_op jit(solution)/shard_map/ppermute | solution.py:247
  7.1 7.4 %collective-permute-start.17 = (bf16[128,1024]{1,0:T(8,128)(2,1)}, bf16[128,1024]{1,0:T(8,128)(2,1)S(1)}, u32[]{:S(2)}, u32[]{:S(2)}) collective-permute-start(bf16[128,1024]{1,0:T(8,128)(2,1)} %refs_2_.2), channel_id=1, source_target_pairs={{0,1},{1,0},{2,3},{3,2},{4,5},{5,4},{6,7},{7,6},{8,9},{9,8},{10,11... | collective-permute-start | bytes 786440 | tf_op jit(solution)/shard_map/ppermute | solution.py:244
  7.1 11.7 %collective-permute-start.13 = (bf16[128,1024]{1,0:T(8,128)(2,1)}, bf16[128,1024]{1,0:T(8,128)(2,1)S(1)}, u32[]{:S(2)}, u32[]{:S(2)}) collective-permute-start(bf16[128,1024]{1,0:T(8,128)(2,1)} %refs_2_.2), channel_id=1, source_target_pairs={{0,4},{4,0},{8,12},{12,8},{1,5},{5,1},{9,13},{13,9},{2,6},{6,2},{1... | collective-permute-start | bytes 786440 | tf_op jit(solution)/shard_map/ppermute | solution.py:248
  10.3 9.9 %collective-permute-start.14 = (bf16[128,1024]{1,0:T(8,128)(2,1)S(1)}, bf16[128,1024]{1,0:T(8,128)(2,1)S(1)}, u32[]{:S(2)}, u32[]{:S(2)}) collective-permute-start(bf16[128,1024]{1,0:T(8,128)(2,1)S(1)} %collective-permute-done.end_ref.refs_1_), channel_id=1, source_target_pairs={{0,1},{1,0},{2,3},{3,2},{4,5},{5,4},{6,7},{7,6},{8,9},{9,8},{10,11... | collective-permute-start | bytes 786440 | tf_op jit(solution)/shard_map/ppermute | solution.py:244
  14.5 24.8 %collective-permute-start.11 = (bf16[256,1024]{1,0:T(8,128)(2,1)}, bf16[256,1024]{1,0:T(8,128)(2,1)S(1)}, u32[]{:S(2)}, u32[]{:S(2)}) collective-permute-start(bf16[256,1024]{1,0:T(8,128)(2,1)} %refs_3_.1), channel_id=1, source_target_pairs={{0,1},{1,0},{2,3},{3,2},{4,5},{5,4},{6,7},{7,6},{8,9},{9,8},{10,11... | collective-permute-start | bytes 1572872 | tf_op jit(solution)/shard_map/ppermute | solution.py:244
  14.5 7.3 %collective-permute-start.16 = (bf16[128,1024]{1,0:T(8,128)(2,1)S(1)}, bf16[128,1024]{1,0:T(8,128)(2,1)S(1)}, u32[]{:S(2)}, u32[]{:S(2)}) collective-permute-start(bf16[128,1024]{1,0:T(8,128)(2,1)S(1)} %collective-permute-done.1.middle_ref.refs_3_), channel_id=1, source_target_pairs={{0,1},{1,0},{2,3},{3,2},{4,5},{5,4},{6,7},{7,6},{8,9},{9,8},{10,11... | collective-permute-start | bytes 786440 | tf_op jit(solution)/shard_map/ppermute | solution.py:244
  18.8 8.3 %collective-permute-start.2 = (bf16[128,1024]{1,0:T(8,128)(2,1)S(1)}, bf16[128,1024]{1,0:T(8,128)(2,1)S(1)}, u32[]{:S(2)}, u32[]{:S(2)}) collective-permute-start(bf16[128,1024]{1,0:T(8,128)(2,1)S(1)} %collective-permute-done.1.middle_ref.refs_3_), channel_id=1, source_target_pairs={{0,2},{1,3},{2,0},{3,1},{4,6},{5,7},{6,4},{7,5},{8,10},{9,11},{10,... | collective-permute-start | bytes 786440 | tf_op jit(solution)/shard_map/ppermute | solution.py:257
  20.3 7.9 %collective-permute-start.15 = (bf16[128,1024]{1,0:T(8,128)(2,1)S(1)}, bf16[128,1024]{1,0:T(8,128)(2,1)S(1)}, u32[]{:S(2)}, u32[]{:S(2)}) collective-permute-start(bf16[128,1024]{1,0:T(8,128)(2,1)S(1)} %collective-permute-done.13.refs_2_), channel_id=1, source_target_pairs={{0,1},{1,0},{2,3},{3,2},{4,5},{5,4},{6,7},{7,6},{8,9},{9,8},{10,11... | collective-permute-start | bytes 786440 | tf_op jit(solution)/shard_map/ppermute | solution.py:244
  20.7 25.1 %collective-permute-start.12 = (bf16[256,1024]{1,0:T(8,128)(2,1)S(1)}, bf16[256,1024]{1,0:T(8,128)(2,1)S(1)}, u32[]{:S(2)}, u32[]{:S(2)}) collective-permute-start(bf16[256,1024]{1,0:T(8,128)(2,1)S(1)} %collective-permute-done.10.refs_4_), channel_id=1, source_target_pairs={{0,1},{1,0},{2,3},{3,2},{4,5},{5,4},{6,7},{7,6},{8,9},{9,8},{10,11... | collective-permute-start | bytes 1572872 | tf_op jit(solution)/shard_map/ppermute | solution.py:244
  20.8 0.9 %copy-start.2 = (bf16[128,1024]{1,0:T(8,128)(2,1)S(1)}, bf16[128,1024]{1,0:T(8,128)(2,1)}, u32[]{:S(2)}) copy-start(bf16[128,1024]{1,0:T(8,128)(2,1)} %refs_2_.2) | copy-start | bytes 786436
  21.8 17.6 %collective-permute-start.6 = (bf16[128,1024]{1,0:T(8,128)(2,1)S(1)}, bf16[128,1024]{1,0:T(8,128)(2,1)S(1)}, u32[]{:S(2)}, u32[]{:S(2)}) collective-permute-start(bf16[128,1024]{1,0:T(8,128)(2,1)S(1)} %shard_map.74), channel_id=1, source_target_pairs={{4,0},{8,12},{12,4},{0,8},{5,1},{9,13},{13,5},{1,9},{6,2},{10,14},... | collective-permute-start | bytes 786440 | tf_op jit(solution)/shard_map/ppermute | solution.py:255
  27.1 12.8 %collective-permute-start.5 = (bf16[128,1024]{1,0:T(8,128)(2,1)S(1)}, bf16[128,1024]{1,0:T(8,128)(2,1)S(1)}, u32[]{:S(2)}, u32[]{:S(2)}) collective-permute-start(bf16[128,1024]{1,0:T(8,128)(2,1)S(1)} %collective-permute-done.end_ref.refs_1_), channel_id=1, source_target_pairs={{0,4},{4,0},{8,12},{12,8},{1,5},{5,1},{9,13},{13,9},{2,6},{6,2},{1... | collective-permute-start | bytes 786440 | tf_op jit(solution)/shard_map/ppermute | solution.py:256
  28.2 17.2 %collective-permute-start.3 = (bf16[128,1024]{1,0:T(8,128)(2,1)S(1)}, bf16[128,1024]{1,0:T(8,128)(2,1)S(1)}, u32[]{:S(2)}, u32[]{:S(2)}) collective-permute-start(bf16[128,1024]{1,0:T(8,128)(2,1)S(1)} %shard_map.73), channel_id=1, source_target_pairs={{4,0},{8,12},{12,4},{0,8},{5,1},{9,13},{13,5},{1,9},{6,2},{10,14},... | collective-permute-start | bytes 786440 | tf_op jit(solution)/shard_map/ppermute | solution.py:266
  32.1 1.2 %copy-start = (bf16[128,4096]{1,0:T(8,128)(2,1)S(1)}, bf16[128,4096]{1,0:T(8,128)(2,1)}, u32[]{:S(2)}) copy-start(bf16[128,4096]{1,0:T(8,128)(2,1)} %refs_1_.5) | copy-start | bytes 3145732
  33.4 0.9 %copy-start.3 = (bf16[128,1024]{1,0:T(8,128)(2,1)S(1)}, bf16[128,1024]{1,0:T(8,128)(2,1)}, u32[]{:S(2)}) copy-start(bf16[128,1024]{1,0:T(8,128)(2,1)} %refs_2_.2) | copy-start | bytes 786436
  39.2 11.3 %collective-permute-start.8 = (bf16[128,1024]{1,0:T(8,128)(2,1)S(1)}, bf16[128,1024]{1,0:T(8,128)(2,1)S(1)}, u32[]{:S(2)}, u32[]{:S(2)}) collective-permute-start(bf16[128,1024]{1,0:T(8,128)(2,1)S(1)} %collective-permute-done.2.middle_ref.refs_2_), channel_id=1, source_target_pairs={{0,1},{1,0},{2,3},{3,2},{4,5},{5,4},{6,7},{7,6},{8,9},{9,8},{10,11... | collective-permute-start | bytes 786440 | tf_op jit(solution)/shard_map/ppermute | solution.py:244
  39.3 11.2 %collective-permute-start.9 = (bf16[128,1024]{1,0:T(8,128)(2,1)S(1)}, bf16[128,1024]{1,0:T(8,128)(2,1)S(1)}, u32[]{:S(2)}, u32[]{:S(2)}) collective-permute-start(bf16[128,1024]{1,0:T(8,128)(2,1)S(1)} %collective-permute-done.6.refs_3_), channel_id=1, source_target_pairs={{0,1},{1,0},{2,3},{3,2},{4,5},{5,4},{6,7},{7,6},{8,9},{9,8},{10,11... | collective-permute-start | bytes 786440 | tf_op jit(solution)/shard_map/ppermute | solution.py:244
  39.8 10.7 %collective-permute-start.7 = (bf16[128,1024]{1,0:T(8,128)(2,1)S(1)}, bf16[128,1024]{1,0:T(8,128)(2,1)S(1)}, u32[]{:S(2)}, u32[]{:S(2)}) collective-permute-start(bf16[128,1024]{1,0:T(8,128)(2,1)S(1)} %collective-permute-done.5.refs_1_), channel_id=1, source_target_pairs={{0,1},{1,0},{2,3},{3,2},{4,5},{5,4},{6,7},{7,6},{8,9},{9,8},{10,11... | collective-permute-start | bytes 786440 | tf_op jit(solution)/shard_map/ppermute | solution.py:244
  39.9 5.9 %copy-start.4 = (bf16[256,1024]{1,0:T(8,128)(2,1)S(1)}, bf16[256,1024]{1,0:T(8,128)(2,1)}, u32[]{:S(2)}) copy-start(bf16[256,1024]{1,0:T(8,128)(2,1)} %refs_3_.1) | copy-start | bytes 1572868
  39.9 5.9 %copy-start.6 = (s32[8]{0:T(128)S(1)}, s32[8]{0:T(128)}, u32[]{:S(2)}) copy-start(s32[8]{0:T(128)} %refs_1_.4) | copy-start | bytes 100
  45.4 10.6 %collective-permute-start.4 = (bf16[128,1024]{1,0:T(8,128)(2,1)S(1)}, bf16[128,1024]{1,0:T(8,128)(2,1)S(1)}, u32[]{:S(2)}, u32[]{:S(2)}) collective-permute-start(bf16[128,1024]{1,0:T(8,128)(2,1)S(1)} %collective-permute-done.3.refs_2_), channel_id=1, source_target_pairs={{0,1},{1,0},{2,3},{3,2},{4,5},{5,4},{6,7},{7,6},{8,9},{9,8},{10,11... | collective-permute-start | bytes 786440 | tf_op jit(solution)/shard_map/ppermute | solution.py:244
  (1 other events, 0.9 us)

commit v4 on v3

v4 whole, which is shorter than its diff:
```python
import functools
import math

import jax
import jax.numpy as jnp
from jax import lax
from jax.experimental import pallas as pl
from jax.experimental.pallas import tpu as pltpu
from jax.sharding import PartitionSpec as P


QH = 32
KVH = 4
DH = 128
BR_DEV = 2
BL = 512


neg_large = -1e30
key_tile = 256
head_block = 4
group_block = 8
kernel_vmem = 28 * 1024 * 1024
vmem = pl.BlockSpec(memory_space=pltpu.VMEM)
smem = pl.BlockSpec(memory_space=pltpu.SMEM)
anywhere = pl.BlockSpec(memory_space=pl.ANY)
hbm = pl.BlockSpec(memory_space=pltpu.HBM)


def tiles_of(spans, scalars):
    tiles, pending, height = [], [], 0
    for kind, refs in spans:
        parts = []
        if kind == "leaf":
            tiles.append(([((refs[0], refs[0]), 0, refs[0].shape[0], None)], True))
        elif kind == "root":
            for ref in refs:
                for start in range(0, ref.shape[0], key_tile):
                    parts.append(((ref, ref), start, min(key_tile, ref.shape[0] - start), None))
        elif kind == "trunk":
            base = scalars["local_branch"] * BL
            for start in range(0, BL, key_tile):
                parts.append(((refs[0], refs[0]), base + start, key_tile, start))
        else:
            rows = refs[0].shape[0]
            place = scalars["core"] if kind[0] == "held" else 1 - scalars["core"]
            parts.append((tuple(refs), 0, rows, (place * 2 + kind[1]) * rows))
        for part in parts:
            pending.append(part)
            height += part[2]
            if height >= key_tile:
                tiles.append((pending, False))
                pending, height = [], 0
    if pending:
        tiles.append((pending, False))
    return tiles


def load(part, lanes, scalars):
    (near, far), start, size, token = part
    if not isinstance(start, int):
        start = pl.multiple_of(start, key_tile)
    rows = near[pl.ds(start, size), lanes]
    if far is not near:
        rows = jnp.where(scalars["elsewhere"], far[pl.ds(start, size), lanes], rows)
    return rows


def joined(parts):
    return parts[0] if len(parts) == 1 else jnp.concatenate(parts, axis=0)


def attend_kernel(kinds, form, *refs):
    refs = list(refs)
    reads_numbers, finishes = form in ("first", "only"), form in ("last", "only")
    masks = any(kind not in ("leaf", "root") for kind, count in kinds)
    if reads_numbers:
        parent_ref, length_ref, live_ref = [refs.pop(0) for _ in range(3)]
        parent = parent_ref[0]
        local_branch = parent - lax.axis_index("branch") * BR_DEV
        length, live_count = length_ref[parent], live_ref[0]
    elif masks or finishes:
        info = refs.pop(0)[...]
        local_branch, length, live_count = [jnp.max(info[number:number + 1]) for number in range(3)]
    query_ref = refs.pop(0)
    spans = [(kind, [refs.pop(0) for _ in range(count)]) for kind, count in kinds]
    carries = not reads_numbers
    if carries:
        old_total, old_max = refs.pop(0), refs.pop(0)
    if finishes:
        out_ref, held_ref, sems = refs
    else:
        total_ref, max_ref = refs.pop(0), refs.pop(0)
    if form == "first":
        info_ref = refs.pop(0)
        row = lax.broadcasted_iota(jnp.int32, info_ref.shape, 0)
        info_ref[...] = jnp.where(row == 0, local_branch, jnp.where(row == 1, length, live_count))
    scalars = {}
    if masks:
        place = lax.axis_index("leaf")
        scalars = dict(
            local_branch=local_branch,
            length=length,
            core=lax.rem(place, 2),
            elsewhere=local_branch != lax.div(place, 2),
        )
        seen_ref = [listed for kind, listed in spans if kind == "root"][0][0]
    tiles = tiles_of(spans, scalars)
    row_count = query_ref.shape[0]
    groups = query_ref.shape[1] // (DH * KVH)
    factor = DH ** -0.5 * math.log2(math.e)

    def lanes_at(number):
        start = number * DH
        return pl.ds(start if isinstance(start, int) else pl.multiple_of(start, DH), DH)

    def head(k, g0):
        total_rows = row_count * group_block
        start = (k * groups + g0) * row_count
        rows = pl.ds(start if isinstance(start, int) else pl.multiple_of(start, row_count), total_rows)
        query = jnp.concatenate(
            [query_ref[:, lanes_at(k * groups + g)] for g in range(g0, g0 + group_block)], axis=0
        )
        if carries:
            total = old_total[rows, :]
            row_max = old_max[rows, :]
        else:
            row_max, total = None, None
        for parts, causal in tiles:
            keys, values, ones = [], [], []
            for part in parts:
                key_rows = load(part, lanes_at(k), scalars)
                value_rows = load(part, lanes_at(KVH + k), scalars)
                one_rows = jnp.ones_like(value_rows)
                if part[3] is not None:
                    used = lax.broadcasted_iota(jnp.int32, key_rows.shape, 0) < scalars["length"] - part[3]
                    seen = seen_ref[:16, lanes_at(k)][:1].astype(jnp.float32)
                    key_rows = jnp.where(used, key_rows.astype(jnp.float32), seen).astype(key_rows.dtype)
                    value_rows = jnp.where(used, value_rows.astype(jnp.float32), 0.0).astype(key_rows.dtype)
                    one_rows = jnp.where(used, 1.0, 0.0).astype(key_rows.dtype)
                keys.append(key_rows)
                values.append(value_rows)
                ones.append(one_rows)
            scores = lax.dot_general(
                query, joined(keys), (((1,), (1,)), ((), ())), preferred_element_type=jnp.float32
            )
            if causal:
                column = lax.broadcasted_iota(jnp.int32, scores.shape, 1)
                row = lax.rem(lax.broadcasted_iota(jnp.int32, scores.shape, 0), row_count)
                scores = jnp.where(column <= row, scores, neg_large)
            top = jnp.broadcast_to(jnp.max(scores, axis=1, keepdims=True), (total_rows, DH))
            new_max = top if row_max is None else jnp.maximum(row_max, top)
            wide = jnp.concatenate([new_max] * (scores.shape[1] // DH), axis=1)
            weights = jnp.exp2((scores - wide) * factor).astype(jnp.bfloat16)
            padded = jnp.concatenate([joined(values), joined(ones)], axis=1)
            product = jnp.dot(weights, padded, preferred_element_type=jnp.float32)
            if total is None:
                total = product
            else:
                shrink = jnp.exp2((row_max - new_max) * factor)
                total = total * jnp.concatenate([shrink, shrink], axis=1) + product
            row_max = new_max
        if finishes:
            result = total[:, :DH] * pl.reciprocal(total[:, DH:])
            live = lax.broadcasted_iota(jnp.int32, (row_count, DH), 0) < live_count
            for g in range(group_block):
                piece = result[g * row_count:(g + 1) * row_count]
                lanes = slice((g0 + g) * DH, (g0 + g + 1) * DH)
                held_ref[k, :, lanes] = jnp.where(live, piece, 0.0).astype(held_ref.dtype)
            if g0 + group_block == groups:
                pltpu.make_async_copy(held_ref.at[k], out_of(out_ref, k), sems.at[k]).start()
        else:
            total_ref[rows, :] = total
            max_ref[rows, :] = row_max

    def out_of(out_ref, k):
        width = groups * DH
        start = k * width
        return out_ref.at[:, pl.ds(start if isinstance(start, int) else pl.multiple_of(start, width), width)]

    def heads(step, unused):
        for extra in range(head_block):
            for g0 in range(0, groups, group_block):
                head(step * head_block + extra, g0)
        return unused

    if head_block == KVH:
        heads(0, 0)
    else:
        lax.fori_loop(0, KVH // head_block, heads, 0)
    if finishes:
        for k in range(KVH):
            pltpu.make_async_copy(held_ref.at[k], out_of(out_ref, k), sems.at[k]).wait()


def attend(form, numbers, queries, spans, state=()):
    row_count = queries.shape[0]
    groups = QH // KVH
    finishes = form in ("last", "only")
    arrays = [array for kind, listed in spans for array in listed]
    operands = [*numbers, queries, *arrays, *state]
    in_specs = [vmem if state else smem] * len(numbers) + [vmem] * (len(operands) - len(numbers))
    state_shape = [jax.ShapeDtypeStruct((KVH * row_count * groups, width), jnp.float32) for width in (2 * DH, DH)]
    scratch, aliases = [], {}
    if finishes:
        out_specs, out_shape = anywhere, jax.ShapeDtypeStruct(queries.shape, queries.dtype)
        scratch = [
            pltpu.VMEM((KVH, row_count, groups * DH), queries.dtype),
            pltpu.SemaphoreType.DMA((KVH,)),
        ]
    else:
        out_specs, out_shape = [vmem, vmem], state_shape
        if form == "first":
            out_specs.append(vmem)
            out_shape.append(jax.ShapeDtypeStruct((8, DH), jnp.int32))
        else:
            aliases = {len(operands) - 2: 0, len(operands) - 1: 1}
    key_count = sum(array.shape[0] for array in arrays)
    return pl.pallas_call(
        functools.partial(attend_kernel, tuple((kind, len(listed)) for kind, listed in spans), form),
        in_specs=in_specs,
        out_specs=out_specs,
        out_shape=out_shape,
        scratch_shapes=scratch,
        input_output_aliases=aliases,
        compiler_params=pltpu.CompilerParams(vmem_limit_bytes=kernel_vmem),
        cost_estimate=pl.CostEstimate(
            flops=4 * row_count * QH * DH * key_count,
            bytes_accessed=2 * row_count * QH * DH * 4,
            transcendentals=row_count * QH * key_count,
        ),
    )(*operands)


def stage_kernel(split, *refs):
    sems = refs[-1]
    copies, at = [], 0
    count = (len(refs) - 1 + split) // 3
    outs = refs[count:-1]
    for number, source in enumerate(refs[:count]):
        height = source.shape[0] if number < split else source.shape[0] // 2
        for start in range(0, source.shape[0], height):
            copies.append(pltpu.make_async_copy(source.at[start:start + height], outs[at], sems.at[at]))
            at += 1
    for copy in copies:
        copy.start()
    for copy in copies:
        copy.wait()


def stage(whole, halved):
    shapes = [jax.ShapeDtypeStruct(array.shape, array.dtype) for array in whole]
    for array in halved:
        shapes += [jax.ShapeDtypeStruct((array.shape[0] // 2, array.shape[1]), array.dtype)] * 2
    arrays = [pltpu.with_memory_space_constraint(array, pltpu.HBM) for array in (*whole, *halved)]
    return pl.pallas_call(
        functools.partial(stage_kernel, len(whole)),
        in_specs=[hbm] * len(arrays),
        out_specs=[vmem] * len(shapes),
        out_shape=shapes,
        scratch_shapes=[pltpu.SemaphoreType.DMA((len(shapes),))],
        compiler_params=pltpu.CompilerParams(vmem_limit_bytes=8 * 1024 * 1024),
    )(*arrays)


def pick_kernel(end_ref, middle_ref, out_ref):
    z = lax.axis_index("branch")
    at_end = (z == 0) | (z == lax.axis_size("branch") - 1)

    @pl.when(at_end)
    def _():
        out_ref[...] = end_ref[...]

    @pl.when(jnp.logical_not(at_end))
    def _():
        out_ref[...] = middle_ref[...]


def pick(end_rows, middle_rows):
    return pl.pallas_call(
        pick_kernel,
        in_specs=[vmem, vmem],
        out_specs=vmem,
        out_shape=jax.ShapeDtypeStruct(end_rows.shape, end_rows.dtype),
        compiler_params=pltpu.CompilerParams(vmem_limit_bytes=4 * 1024 * 1024),
    )(end_rows, middle_rows)


def gathered_body(queries, leaf_kv, branch_kv, root_kv, branch_len, leaf_len, leaf_parent):
    trunk_rows = lax.all_gather(branch_kv, "leaf", axis=0, tiled=True)
    whole_root = lax.all_gather(root_kv, ("branch", "leaf"), axis=0, tiled=True)
    numbers = (leaf_parent, branch_len, leaf_len)
    spans = [("leaf", [leaf_kv]), ("trunk", [trunk_rows]), ("root", [whole_root])]
    return attend("only", numbers, queries, spans)


def exchanged_body(queries, leaf_kv, branch_kv, root_kv, branch_len, leaf_len, leaf_parent):
    across = [(i, i ^ 2) for i in range(4)]
    beside = [(i, i ^ 1) for i in range(4)]
    near = [(i, i ^ 1) for i in range(4)]
    far = [(i, i ^ 3) for i in range(4)]
    cross = [(1, 0), (2, 3), (3, 1), (0, 2)]
    numbers = (leaf_parent, branch_len, leaf_len)

    def swap(rows):
        return lax.ppermute(rows, "leaf", beside)

    far_own = lax.ppermute(root_kv, "branch", far)
    near_own = lax.ppermute(root_kv, "branch", near)
    side = lax.ppermute(root_kv, "leaf", across)
    own_swapped = swap(root_kv)
    kept, own_leaf, own, low, high = stage((queries, leaf_kv, root_kv), (branch_kv,))
    low_side = lax.ppermute(low, "leaf", across)
    high_side = lax.ppermute(high, "leaf", across)
    low_swapped = swap(low)
    high_swapped = swap(high)
    *state, info = attend("first", numbers, kept, [("leaf", [own_leaf]), ("root", [own, own_swapped])])

    near_side = lax.ppermute(side, "branch", near)
    far_side = lax.ppermute(far_own, "leaf", across)
    cross_own = lax.ppermute(pick(own, far_own), "branch", cross)
    side_swapped = swap(side)
    near_own_swapped = swap(near_own)
    far_own_swapped = swap(far_own)
    low_side_swapped = swap(low_side)
    state = attend("middle", (), kept, [
        ("root", [side, near_own, far_own, side_swapped, near_own_swapped, far_own_swapped]),
    ], state)

    cross_side = lax.ppermute(pick(side, far_side), "branch", cross)
    near_side_swapped = swap(near_side)
    far_side_swapped = swap(far_side)
    state = attend("middle", (info,), kept, [
        (("held", 0), [low, low_side]),
        (("swapped", 0), [low_swapped, low_side_swapped]),
        ("root", [near_side, far_side, near_side_swapped, far_side_swapped]),
    ], state)

    cross_own_swapped = swap(cross_own)
    high_side_swapped = swap(high_side)
    cross_side_swapped = swap(cross_side)
    state = attend("middle", (info,), kept, [
        (("held", 1), [high, high_side]),
        (("swapped", 1), [high_swapped, high_side_swapped]),
        ("root", [cross_own, cross_own_swapped]),
    ], state)
    return attend("last", (info,), kept, [("root", [cross_side, cross_side_swapped])], state)


def solution(mesh):
    split = P(("rep", "branch", "leaf"), None)
    single = P(("rep", "branch", "leaf"))
    small = mesh.shape["branch"] == 4 and mesh.shape["leaf"] == 4
    return jax.shard_map(
        exchanged_body if small else gathered_body,
        mesh=mesh,
        in_specs=(split, split, split, split, P("rep"), single, single),
        out_specs=split,
        check_vma=False,
    )
```

time: 59.7 us -> 53.6 us (0.90)
  local copies, waits for them, and re-layouts: 4.08 us -> 0.65 us
  Pallas kernels: 22.9 us -> 20.4 us
    pallas_call x5, Pallas kernels: 22.9 us -> 18.8 us  [attend(): pl.pallas_call(functools.partial(attend_kernel, tuple(((kind, len(listed)...]
    unnamed x14 -> x2, local copies, waits for them, and re-layouts: 4.08 us -> 0.65 us
    ppermute x4 -> x5, starting transfers between devices: 7.11 us -> 8.89 us  [the longest x1 3.6 us: exchanged_body(): far_own = lax.ppermute(root_kv, 'branch', far)]
    pallas_call x0 -> x1, Pallas kernels: none -> 1.54 us  [stage(): pl.pallas_call(functools.partial(stage_kernel, len(whole)), in_specs=[hbm...]
    ppermute x4 -> x5, waiting for transfers between devices: 11.6 us -> 10.3 us  [the longest x1 4.98 us: exchanged_body(): near_own = lax.ppermute(root_kv, 'branch', near)]
    ppermute x1, waiting for transfers between devices: 0.01 us -> 1.21 us  [exchanged_body(): near_side = lax.ppermute(side, 'branch', near)]
    ppermute x1, starting transfers between devices: 3.79 us -> 2.61 us  [exchanged_body(): cross_own = lax.ppermute(pick(own, far_own), 'branch', cross)]
    ppermute x1, starting transfers between devices: 1.49 us -> 0.54 us  [exchanged_body(): far_side = lax.ppermute(far_own, 'leaf', across)]
  transfers between devices with their start and end apart: 18 -> 21, of which waited for: 5 -> 6; matrix products, arithmetic and copies ran while one was open for 0% -> 0% of each run, Pallas kernels for 33% -> 33%
where the time goes in v4:
time: 53.6 us; the launch traced here: 53.4 us
  Pallas kernels  20.4 us (38%)
  starting transfers between devices  17.8 us (33%)
  waiting for transfers between devices  13 us (24%)
  between operations  1.61 us (3%)
  local copies, waits for them, and re-layouts  0.65 us (1%)
    pallas_call x5, Pallas kernels, attend(): pl.pallas_call(functools.partial(attend_kernel, tuple(((kind, len(listed)...  18.8 us
    ppermute x1, waiting for transfers between devices, exchanged_body(): near_own = lax.ppermute(root_kv, 'branch', near)  4.98 us
    ppermute x1, starting transfers between devices, exchanged_body(): far_own = lax.ppermute(root_kv, 'branch', far)  3.6 us
    ppermute x1, starting transfers between devices, exchanged_body(): cross_own = lax.ppermute(pick(own, far_own), 'branch', cross)  2.61 us
    ppermute x1, starting transfers between devices, exchanged_body(): side = lax.ppermute(root_kv, 'leaf', across)  2.48 us
    ppermute x1, starting transfers between devices, exchanged_body(): high_side = lax.ppermute(high, 'leaf', across)  2.2 us
    ppermute x12, starting transfers between devices, swap(): return lax.ppermute(rows, 'leaf', beside)  2.04 us
    ppermute x1, waiting for transfers between devices, exchanged_body(): high_side = lax.ppermute(high, 'leaf', across)  1.96 us
  transfers between devices with their start and end apart: 21, of which 6 were waited for; matrix products, arithmetic and copies ran while one was open for 0% of the time, Pallas kernels for 33%

profile of v4, /device:TPU:0, one launch (start us, length us, event | category | flops | bytes accessed | tf_op | source)
XLA Modules:
  0.0 53.4 jit_solution(17666731275377267713)
XLA Ops:
  0.0 0.5 collective-permute-start
  0.5 2.5 %collective-permute-start.1 = (bf16[128,1024]{1,0:T(8,128)(2,1)}, bf16[128,1024]{1,0:T(8,128)(2,1)S(1)}, u32[]{:S(2)}, u32[]{:S(2)}) collective-permute-start(bf16[128,1024]{1,0:T(8,128)(2,1)} %refs_2_.2), channel_id=1, source_target_pairs={{0,2},{1,3},{2,0},{3,1},{4,6},{5,7},{6,4},{7,5},{8,10},{9,11},{10,... | collective-permute-start | bytes 786440 | tf_op jit(solution)/shard_map/ppermute | solution.py:310
  3.0 3.6 %collective-permute-start.2 = (bf16[128,1024]{1,0:T(8,128)(2,1)}, bf16[128,1024]{1,0:T(8,128)(2,1)S(1)}, u32[]{:S(2)}, u32[]{:S(2)}) collective-permute-start(bf16[128,1024]{1,0:T(8,128)(2,1)} %refs_2_.2), channel_id=1, source_target_pairs={{0,12},{4,8},{8,4},{12,0},{1,13},{5,9},{9,5},{13,1},{2,14},{6,10},... | collective-permute-start | bytes 786440 | tf_op jit(solution)/shard_map/ppermute | solution.py:308
  6.6 1.5 %shard_map.73 = (bf16[128,4096]{1,0:T(8,128)(2,1)S(1)}, bf16[128,1024]{1,0:T(8,128)(2,1)S(1)}, bf16[128,1024]{1,0:T(8,128)(2,1)S(1)}, bf16[128,1024]{1,0:T(8,128)(2,1)S(1)}, bf16[128,1024]{1,0:T(8,128)(2,1)S(1)}) custom-call(bf16[128,4096]{1,0:T(8,128)(2,1)} %refs_0_.2, bf16[128,1024]{1,0:T(8,128)(2,1)} %refs_1_.2, bf16[128,1024]{1,0:T(8,128)(2,1)} %refs_2_.2, ...), custom_call_target="tpu_custom_call" | custom-call | tf_op jit(solution)/shard_map/pallas_call | solution.py:256
  8.1 0.6 %collective-permute-start.11 = (bf16[128,1024]{1,0:T(8,128)(2,1)S(1)}, bf16[128,1024]{1,0:T(8,128)(2,1)S(1)}, u32[]{:S(2)}, u32[]{:S(2)}) collective-permute-start(bf16[128,1024]{1,0:T(8,128)(2,1)S(1)} %get-tuple-element.24.refs_2_), channel_id=1, source_target_pairs={{0,2},{1,3},{2,0},{3,1},{4,6},{5,7},{6,4},{7,5},{8,10},{9,11},{10,... | collective-permute-start | bytes 786440 | tf_op jit(solution)/shard_map/ppermute | solution.py:313
  8.7 1.4 %collective-permute-done.1.end_ref.refs_1_ = bf16[128,1024]{1,0:T(8,128)(2,1)S(1)} collective-permute-done((bf16[128,1024]{1,0:T(8,128)(2,1)}, bf16[128,1024]{1,0:T(8,128)(2,1)S(1)}, u32[]{:S(2)}, u32[]{:S(2)}) %collective-permute-start.1) | collective-permute-done | bytes 262176 | tf_op jit(solution)/shard_map/ppermute | solution.py:310
  10.2 2.2 %collective-permute-start.6 = (bf16[128,1024]{1,0:T(8,128)(2,1)S(1)}, bf16[128,1024]{1,0:T(8,128)(2,1)S(1)}, u32[]{:S(2)}, u32[]{:S(2)}) collective-permute-start(bf16[128,1024]{1,0:T(8,128)(2,1)S(1)} %get-tuple-element.23.refs_2_), channel_id=1, source_target_pairs={{0,2},{1,3},{2,0},{3,1},{4,6},{5,7},{6,4},{7,5},{8,10},{9,11},{10,... | collective-permute-start | bytes 786440 | tf_op jit(solution)/shard_map/ppermute | solution.py:314
  12.4 1.9 %collective-permute-done.2.middle_ref.refs_3_ = bf16[128,1024]{1,0:T(8,128)(2,1)S(1)} collective-permute-done((bf16[128,1024]{1,0:T(8,128)(2,1)}, bf16[128,1024]{1,0:T(8,128)(2,1)S(1)}, u32[]{:S(2)}, u32[]{:S(2)}) %collective-permute-start.2) | collective-permute-done | bytes 262176 | tf_op jit(solution)/shard_map/ppermute | solution.py:308
  14.3 5.0 %collective-permute-done.17.refs_2_ = bf16[128,1024]{1,0:T(8,128)(2,1)S(1)} collective-permute-done((bf16[128,1024]{1,0:T(8,128)(2,1)}, bf16[128,1024]{1,0:T(8,128)(2,1)S(1)}, u32[]{:S(2)}, u32[]{:S(2)}) %collective-permute-start.17) | collective-permute-done | bytes 262176 | tf_op jit(solution)/shard_map/ppermute | solution.py:309
  19.3 0.5 %collective-permute-start.3 = (bf16[128,1024]{1,0:T(8,128)(2,1)S(1)}, bf16[128,1024]{1,0:T(8,128)(2,1)S(1)}, u32[]{:S(2)}, u32[]{:S(2)}) collective-permute-start(bf16[128,1024]{1,0:T(8,128)(2,1)S(1)} %collective-permute-done.2.middle_ref.refs_3_), channel_id=1, source_target_pairs={{0,2},{1,3},{2,0},{3,1},{4,6},{5,7},{6,4},{7,5},{8,10},{9,11},{10,... | collective-permute-start | bytes 786440 | tf_op jit(solution)/shard_map/ppermute | solution.py:320
  20.0 2.0 %collective-permute-done.6.refs_3_ = bf16[128,1024]{1,0:T(8,128)(2,1)S(1)} collective-permute-done((bf16[128,1024]{1,0:T(8,128)(2,1)S(1)}, bf16[128,1024]{1,0:T(8,128)(2,1)S(1)}, u32[]{:S(2)}, u32[]{:S(2)}) %collective-permute-start.6) | collective-permute-done | bytes 262176 | tf_op jit(solution)/shard_map/ppermute | solution.py:314
  22.0 1.7 %collective-permute-start.14 = (bf16[128,1024]{1,0:T(8,128)(2,1)S(1)}, bf16[128,1024]{1,0:T(8,128)(2,1)S(1)}, u32[]{:S(2)}, u32[]{:S(2)}) collective-permute-start(bf16[128,1024]{1,0:T(8,128)(2,1)S(1)} %collective-permute-done.1.end_ref.refs_1_), channel_id=1, source_target_pairs={{0,4},{4,0},{8,12},{12,8},{1,5},{5,1},{9,13},{13,9},{2,6},{6,2},{1... | collective-permute-start | bytes 786440 | tf_op jit(solution)/shard_map/ppermute | solution.py:319
  23.8 2.6 %collective-permute-start.9 = (bf16[128,1024]{1,0:T(8,128)(2,1)S(1)}, bf16[128,1024]{1,0:T(8,128)(2,1)S(1)}, u32[]{:S(2)}, u32[]{:S(2)}) collective-permute-start(bf16[128,1024]{1,0:T(8,128)(2,1)S(1)} %shard_map.76), channel_id=1, source_target_pairs={{4,0},{8,12},{12,4},{0,8},{5,1},{9,13},{13,5},{1,9},{6,2},{10,14},... | collective-permute-start | bytes 786440 | tf_op jit(solution)/shard_map/ppermute | solution.py:321
  26.4 1.5 %collective-permute-done.3.middle_ref.refs_7_ = bf16[128,1024]{1,0:T(8,128)(2,1)S(1)} collective-permute-done((bf16[128,1024]{1,0:T(8,128)(2,1)S(1)}, bf16[128,1024]{1,0:T(8,128)(2,1)S(1)}, u32[]{:S(2)}, u32[]{:S(2)}) %collective-permute-start.3) | collective-permute-done | bytes 262176 | tf_op jit(solution)/shard_map/ppermute | solution.py:320
  28.0 1.9 %collective-permute-start.4 = (bf16[128,1024]{1,0:T(8,128)(2,1)S(1)}, bf16[128,1024]{1,0:T(8,128)(2,1)S(1)}, u32[]{:S(2)}, u32[]{:S(2)}) collective-permute-start(bf16[128,1024]{1,0:T(8,128)(2,1)S(1)} %shard_map.75), channel_id=1, source_target_pairs={{4,0},{8,12},{12,4},{0,8},{5,1},{9,13},{13,5},{1,9},{6,2},{10,14},... | collective-permute-start | bytes 786440 | tf_op jit(solution)/shard_map/ppermute | solution.py:330
  29.9 1.2 %collective-permute-done.14.refs_6_ = bf16[128,1024]{1,0:T(8,128)(2,1)S(1)} collective-permute-done((bf16[128,1024]{1,0:T(8,128)(2,1)S(1)}, bf16[128,1024]{1,0:T(8,128)(2,1)S(1)}, u32[]{:S(2)}, u32[]{:S(2)}) %collective-permute-start.14) | collective-permute-done | bytes 262176 | tf_op jit(solution)/shard_map/ppermute | solution.py:319
  32.5 0.6 %copy-done = s32[8]{0:T(128)S(1)} copy-done((s32[8]{0:T(128)S(1)}, s32[8]{0:T(128)}, u32[]{:S(2)}) %copy-start) | copy-done | bytes 56
  33.1 3.3 %shard_map.74 = (f32[4096,256]{1,0:T(8,128)S(1)}, f32[4096,128]{1,0:T(8,128)S(1)}, s32[8,128]{1,0:T(8,128)S(1)}) custom-call(s32[1]{0:T(128)S(6)} %copy.21.refs_0_, s32[8]{0:T(128)S(1)} %copy-done, s32[1]{0:T(128)S(6)} %copy.20.refs_2_, bf16[128,4096]{1,0:T(8,128)(2,1)S(1)} %get-tuple-element.19.refs_3_.refs_0_.refs_1_, ...), custom_call_target="tpu_custom_call" | custom-call | flops 805306368 | bytes 4194304 | tf_op jit(solution)/shard_map/pallas_call | solution.py:219
  36.5 0.6 %collective-permute-start.7 = (bf16[128,1024]{1,0:T(8,128)(2,1)S(1)}, bf16[128,1024]{1,0:T(8,128)(2,1)S(1)}, u32[]{:S(2)}, u32[]{:S(2)}) collective-permute-start(bf16[128,1024]{1,0:T(8,128)(2,1)S(1)} %get-tuple-element.23.refs_2_), channel_id=1, source_target_pairs={{0,1},{1,0},{2,3},{3,2},{4,5},{5,4},{6,7},{7,6},{8,9},{9,8},{10,11... | collective-permute-start | bytes 786440 | tf_op jit(solution)/shard_map/ppermute | solution.py:306
  37.1 0.4 collective-permute-start.10
  37.6 4.2 %shard_map.77 = (f32[4096,256]{1,0:T(8,128)S(1)}, f32[4096,128]{1,0:T(8,128)S(1)}) custom-call(bf16[128,4096]{1,0:T(8,128)(2,1)S(1)} %get-tuple-element.19.refs_3_.refs_0_.refs_1_, bf16[128,1024]{1,0:T(8,128)(2,1)S(1)} %collective-permute-done.1.end_ref.refs_1_, ...), custom_call_target="tpu_custom_call", output_to_operand_aliasing={{0}: (7, {}), {1}: (8, {})} | custom-call | flops 1610612736 | bytes 4194304 | tf_op jit(solution)/shard_map/pallas_call | solution.py:219
  41.9 4.5 %shard_map.78 = (f32[4096,256]{1,0:T(8,128)S(1)}, f32[4096,128]{1,0:T(8,128)S(1)}) custom-call(s32[8,128]{1,0:T(8,128)S(1)} %get-tuple-element.22.refs_0_, bf16[128,4096]{1,0:T(8,128)(2,1)S(1)} %get-tuple-element.19.refs_3_.refs_0_.refs_1_, bf16[128,1024]{1,0:T(8,128)(2,1)S(1)} %get-tuple-element.24.refs_2_, ...), custom_call_target="tpu_custom_call", output_to_operand_aliasing={{0}: (10, {}), {1}: (11, {})} | custom-call | flops 2147483648 | bytes 4194304 | tf_op jit(solution)/shard_map/pallas_call | solution.py:219
  46.5 3.9 %shard_map.79 = (f32[4096,256]{1,0:T(8,128)S(1)}, f32[4096,128]{1,0:T(8,128)S(1)}) custom-call(s32[8,128]{1,0:T(8,128)S(1)} %get-tuple-element.22.refs_0_, bf16[128,4096]{1,0:T(8,128)(2,1)S(1)} %get-tuple-element.19.refs_3_.refs_0_.refs_1_, bf16[128,1024]{1,0:T(8,128)(2,1)S(1)} %get-tuple-element.23.refs_2_, ...), custom_call_target="tpu_custom_call", output_to_operand_aliasing={{0}: (8, {}), {1}: (9, {})} | custom-call | flops 1610612736 | bytes 4194304 | tf_op jit(solution)/shard_map/pallas_call | solution.py:219
  50.3 2.9 %shard_map.80 = bf16[128,4096]{1,0:T(8,128)(2,1)} custom-call(s32[8,128]{1,0:T(8,128)S(1)} %get-tuple-element.22.refs_0_, bf16[128,4096]{1,0:T(8,128)(2,1)S(1)} %get-tuple-element.19.refs_3_.refs_0_.refs_1_, bf16[128,1024]{1,0:T(8,128)(2,1)S(1)} %collective-permute-done.4.refs_2_, bf16[128,1024]{1,0:T(8,128)(2,1)S(1)} %collective-permute-done.5.refs_3_, ...), custom_call_target="tpu_custom_call" | custom-call | flops 536870912 | bytes 4194304 | tf_op jit(solution)/shard_map/pallas_call | solution.py:219
  (28 shorter events, 0.6 us)
Async XLA Ops:
  0.0 8.7 %collective-permute-start = (bf16[128,1024]{1,0:T(8,128)(2,1)}, bf16[128,1024]{1,0:T(8,128)(2,1)S(1)}, u32[]{:S(2)}, u32[]{:S(2)}) collective-permute-start(bf16[128,1024]{1,0:T(8,128)(2,1)} %refs_2_.2), channel_id=1, source_target_pairs={{0,1},{1,0},{2,3},{3,2},{4,5},{5,4},{6,7},{7,6},{8,9},{9,8},{10,11... | collective-permute-start | bytes 786440 | tf_op jit(solution)/shard_map/ppermute | solution.py:306
  0.5 9.7 %collective-permute-start.1 = (bf16[128,1024]{1,0:T(8,128)(2,1)}, bf16[128,1024]{1,0:T(8,128)(2,1)S(1)}, u32[]{:S(2)}, u32[]{:S(2)}) collective-permute-start(bf16[128,1024]{1,0:T(8,128)(2,1)} %refs_2_.2), channel_id=1, source_target_pairs={{0,2},{1,3},{2,0},{3,1},{4,6},{5,7},{6,4},{7,5},{8,10},{9,11},{10,... | collective-permute-start | bytes 786440 | tf_op jit(solution)/shard_map/ppermute | solution.py:310
  3.0 11.3 %collective-permute-start.2 = (bf16[128,1024]{1,0:T(8,128)(2,1)}, bf16[128,1024]{1,0:T(8,128)(2,1)S(1)}, u32[]{:S(2)}, u32[]{:S(2)}) collective-permute-start(bf16[128,1024]{1,0:T(8,128)(2,1)} %refs_2_.2), channel_id=1, source_target_pairs={{0,12},{4,8},{8,4},{12,0},{1,13},{5,9},{9,5},{13,1},{2,14},{6,10},... | collective-permute-start | bytes 786440 | tf_op jit(solution)/shard_map/ppermute | solution.py:308
  6.6 12.7 %collective-permute-start.17 = (bf16[128,1024]{1,0:T(8,128)(2,1)}, bf16[128,1024]{1,0:T(8,128)(2,1)S(1)}, u32[]{:S(2)}, u32[]{:S(2)}) collective-permute-start(bf16[128,1024]{1,0:T(8,128)(2,1)} %refs_2_.2), channel_id=1, source_target_pairs={{0,4},{4,0},{8,12},{12,8},{1,5},{5,1},{9,13},{13,9},{2,6},{6,2},{1... | collective-permute-start | bytes 786440 | tf_op jit(solution)/shard_map/ppermute | solution.py:309
  8.1 11.1 %collective-permute-start.11 = (bf16[128,1024]{1,0:T(8,128)(2,1)S(1)}, bf16[128,1024]{1,0:T(8,128)(2,1)S(1)}, u32[]{:S(2)}, u32[]{:S(2)}) collective-permute-start(bf16[128,1024]{1,0:T(8,128)(2,1)S(1)} %get-tuple-element.24.refs_2_), channel_id=1, source_target_pairs={{0,2},{1,3},{2,0},{3,1},{4,6},{5,7},{6,4},{7,5},{8,10},{9,11},{10,... | collective-permute-start | bytes 786440 | tf_op jit(solution)/shard_map/ppermute | solution.py:313
  8.7 11.1 %collective-permute-start.12 = (bf16[128,1024]{1,0:T(8,128)(2,1)S(1)}, bf16[128,1024]{1,0:T(8,128)(2,1)S(1)}, u32[]{:S(2)}, u32[]{:S(2)}) collective-permute-start(bf16[128,1024]{1,0:T(8,128)(2,1)S(1)} %get-tuple-element.24.refs_2_), channel_id=1, source_target_pairs={{0,1},{1,0},{2,3},{3,2},{4,5},{5,4},{6,7},{7,6},{8,9},{9,8},{10,11... | collective-permute-start | bytes 786440 | tf_op jit(solution)/shard_map/ppermute | solution.py:306
  10.2 11.8 %collective-permute-start.6 = (bf16[128,1024]{1,0:T(8,128)(2,1)S(1)}, bf16[128,1024]{1,0:T(8,128)(2,1)S(1)}, u32[]{:S(2)}, u32[]{:S(2)}) collective-permute-start(bf16[128,1024]{1,0:T(8,128)(2,1)S(1)} %get-tuple-element.23.refs_2_), channel_id=1, source_target_pairs={{0,2},{1,3},{2,0},{3,1},{4,6},{5,7},{6,4},{7,5},{8,10},{9,11},{10,... | collective-permute-start | bytes 786440 | tf_op jit(solution)/shard_map/ppermute | solution.py:314
  14.3 9.5 %collective-permute-start.18 = (bf16[128,1024]{1,0:T(8,128)(2,1)S(1)}, bf16[128,1024]{1,0:T(8,128)(2,1)S(1)}, u32[]{:S(2)}, u32[]{:S(2)}) collective-permute-start(bf16[128,1024]{1,0:T(8,128)(2,1)S(1)} %collective-permute-done.1.end_ref.refs_1_), channel_id=1, source_target_pairs={{0,1},{1,0},{2,3},{3,2},{4,5},{5,4},{6,7},{7,6},{8,9},{9,8},{10,11... | collective-permute-start | bytes 786440 | tf_op jit(solution)/shard_map/ppermute | solution.py:306
  19.2 4.6 %collective-permute-start.20 = (bf16[128,1024]{1,0:T(8,128)(2,1)S(1)}, bf16[128,1024]{1,0:T(8,128)(2,1)S(1)}, u32[]{:S(2)}, u32[]{:S(2)}) collective-permute-start(bf16[128,1024]{1,0:T(8,128)(2,1)S(1)} %collective-permute-done.2.middle_ref.refs_3_), channel_id=1, source_target_pairs={{0,1},{1,0},{2,3},{3,2},{4,5},{5,4},{6,7},{7,6},{8,9},{9,8},{10,11... | collective-permute-start | bytes 786440 | tf_op jit(solution)/shard_map/ppermute | solution.py:306
  19.3 8.7 %collective-permute-start.3 = (bf16[128,1024]{1,0:T(8,128)(2,1)S(1)}, bf16[128,1024]{1,0:T(8,128)(2,1)S(1)}, u32[]{:S(2)}, u32[]{:S(2)}) collective-permute-start(bf16[128,1024]{1,0:T(8,128)(2,1)S(1)} %collective-permute-done.2.middle_ref.refs_3_), channel_id=1, source_target_pairs={{0,2},{1,3},{2,0},{3,1},{4,6},{5,7},{6,4},{7,5},{8,10},{9,11},{10,... | collective-permute-start | bytes 786440 | tf_op jit(solution)/shard_map/ppermute | solution.py:320
  19.8 8.2 %collective-permute-start.19 = (bf16[128,1024]{1,0:T(8,128)(2,1)S(1)}, bf16[128,1024]{1,0:T(8,128)(2,1)S(1)}, u32[]{:S(2)}, u32[]{:S(2)}) collective-permute-start(bf16[128,1024]{1,0:T(8,128)(2,1)S(1)} %collective-permute-done.17.refs_2_), channel_id=1, source_target_pairs={{0,1},{1,0},{2,3},{3,2},{4,5},{5,4},{6,7},{7,6},{8,9},{9,8},{10,11... | collective-permute-start | bytes 786440 | tf_op jit(solution)/shard_map/ppermute | solution.py:306
  22.0 9.2 %collective-permute-start.14 = (bf16[128,1024]{1,0:T(8,128)(2,1)S(1)}, bf16[128,1024]{1,0:T(8,128)(2,1)S(1)}, u32[]{:S(2)}, u32[]{:S(2)}) collective-permute-start(bf16[128,1024]{1,0:T(8,128)(2,1)S(1)} %collective-permute-done.1.end_ref.refs_1_), channel_id=1, source_target_pairs={{0,4},{4,0},{8,12},{12,8},{1,5},{5,1},{9,13},{13,9},{2,6},{6,2},{1... | collective-permute-start | bytes 786440 | tf_op jit(solution)/shard_map/ppermute | solution.py:319
  23.7 12.7 %collective-permute-start.13 = (bf16[128,1024]{1,0:T(8,128)(2,1)S(1)}, bf16[128,1024]{1,0:T(8,128)(2,1)S(1)}, u32[]{:S(2)}, u32[]{:S(2)}) collective-permute-start(bf16[128,1024]{1,0:T(8,128)(2,1)S(1)} %collective-permute-done.11.refs_3_), channel_id=1, source_target_pairs={{0,1},{1,0},{2,3},{3,2},{4,5},{5,4},{6,7},{7,6},{8,9},{9,8},{10,11... | collective-permute-start | bytes 786440 | tf_op jit(solution)/shard_map/ppermute | solution.py:306
  23.8 13.2 %collective-permute-start.9 = (bf16[128,1024]{1,0:T(8,128)(2,1)S(1)}, bf16[128,1024]{1,0:T(8,128)(2,1)S(1)}, u32[]{:S(2)}, u32[]{:S(2)}) collective-permute-start(bf16[128,1024]{1,0:T(8,128)(2,1)S(1)} %shard_map.76), channel_id=1, source_target_pairs={{4,0},{8,12},{12,4},{0,8},{5,1},{9,13},{13,5},{1,9},{6,2},{10,14},... | collective-permute-start | bytes 786440 | tf_op jit(solution)/shard_map/ppermute | solution.py:321
  28.0 9.2 %collective-permute-start.16 = (bf16[128,1024]{1,0:T(8,128)(2,1)S(1)}, bf16[128,1024]{1,0:T(8,128)(2,1)S(1)}, u32[]{:S(2)}, u32[]{:S(2)}) collective-permute-start(bf16[128,1024]{1,0:T(8,128)(2,1)S(1)} %collective-permute-done.3.middle_ref.refs_7_), channel_id=1, source_target_pairs={{0,1},{1,0},{2,3},{3,2},{4,5},{5,4},{6,7},{7,6},{8,9},{9,8},{10,11... | collective-permute-start | bytes 786440 | tf_op jit(solution)/shard_map/ppermute | solution.py:306
  28.0 13.8 %collective-permute-start.4 = (bf16[128,1024]{1,0:T(8,128)(2,1)S(1)}, bf16[128,1024]{1,0:T(8,128)(2,1)S(1)}, u32[]{:S(2)}, u32[]{:S(2)}) collective-permute-start(bf16[128,1024]{1,0:T(8,128)(2,1)S(1)} %shard_map.75), channel_id=1, source_target_pairs={{4,0},{8,12},{12,4},{0,8},{5,1},{9,13},{13,5},{1,9},{6,2},{10,14},... | collective-permute-start | bytes 786440 | tf_op jit(solution)/shard_map/ppermute | solution.py:330
  31.1 10.8 %collective-permute-start.15 = (bf16[128,1024]{1,0:T(8,128)(2,1)S(1)}, bf16[128,1024]{1,0:T(8,128)(2,1)S(1)}, u32[]{:S(2)}, u32[]{:S(2)}) collective-permute-start(bf16[128,1024]{1,0:T(8,128)(2,1)S(1)} %collective-permute-done.14.refs_6_), channel_id=1, source_target_pairs={{0,1},{1,0},{2,3},{3,2},{4,5},{5,4},{6,7},{7,6},{8,9},{9,8},{10,11... | collective-permute-start | bytes 786440 | tf_op jit(solution)/shard_map/ppermute | solution.py:306
  32.5 0.7 %copy-start = (s32[8]{0:T(128)S(1)}, s32[8]{0:T(128)}, u32[]{:S(2)}) copy-start(s32[8]{0:T(128)} %refs_1_.3) | copy-start | bytes 100
  36.5 10.0 %collective-permute-start.7 = (bf16[128,1024]{1,0:T(8,128)(2,1)S(1)}, bf16[128,1024]{1,0:T(8,128)(2,1)S(1)}, u32[]{:S(2)}, u32[]{:S(2)}) collective-permute-start(bf16[128,1024]{1,0:T(8,128)(2,1)S(1)} %get-tuple-element.23.refs_2_), channel_id=1, source_target_pairs={{0,1},{1,0},{2,3},{3,2},{4,5},{5,4},{6,7},{7,6},{8,9},{9,8},{10,11... | collective-permute-start | bytes 786440 | tf_op jit(solution)/shard_map/ppermute | solution.py:306
  37.0 9.4 %collective-permute-start.8 = (bf16[128,1024]{1,0:T(8,128)(2,1)S(1)}, bf16[128,1024]{1,0:T(8,128)(2,1)S(1)}, u32[]{:S(2)}, u32[]{:S(2)}) collective-permute-start(bf16[128,1024]{1,0:T(8,128)(2,1)S(1)} %collective-permute-done.6.refs_3_), channel_id=1, source_target_pairs={{0,1},{1,0},{2,3},{3,2},{4,5},{5,4},{6,7},{7,6},{8,9},{9,8},{10,11... | collective-permute-start | bytes 786440 | tf_op jit(solution)/shard_map/ppermute | solution.py:306
  37.1 9.3 %collective-permute-start.10 = (bf16[128,1024]{1,0:T(8,128)(2,1)S(1)}, bf16[128,1024]{1,0:T(8,128)(2,1)S(1)}, u32[]{:S(2)}, u32[]{:S(2)}) collective-permute-start(bf16[128,1024]{1,0:T(8,128)(2,1)S(1)} %collective-permute-done.9.refs_6_), channel_id=1, source_target_pairs={{0,1},{1,0},{2,3},{3,2},{4,5},{5,4},{6,7},{7,6},{8,9},{9,8},{10,11... | collective-permute-start | bytes 786440 | tf_op jit(solution)/shard_map/ppermute | solution.py:306
  41.8 8.6 %collective-permute-start.5 = (bf16[128,1024]{1,0:T(8,128)(2,1)S(1)}, bf16[128,1024]{1,0:T(8,128)(2,1)S(1)}, u32[]{:S(2)}, u32[]{:S(2)}) collective-permute-start(bf16[128,1024]{1,0:T(8,128)(2,1)S(1)} %collective-permute-done.4.refs_2_), channel_id=1, source_target_pairs={{0,1},{1,0},{2,3},{3,2},{4,5},{5,4},{6,7},{7,6},{8,9},{9,8},{10,11... | collective-permute-start | bytes 786440 | tf_op jit(solution)/shard_map/ppermute | solution.py:306

commit v5 on v4

--- a/solution.py
+++ b/solution.py
@@ -1,5 +1,6 @@
 import functools
 import math
+import types
 
 import jax
 import jax.numpy as jnp
@@ -38,12 +39,12 @@
                 for start in range(0, ref.shape[0], key_tile):
                     parts.append(((ref, ref), start, min(key_tile, ref.shape[0] - start), None))
         elif kind == "trunk":
-            base = scalars["local_branch"] * BL
+            base = scalars.local_branch * BL
             for start in range(0, BL, key_tile):
                 parts.append(((refs[0], refs[0]), base + start, key_tile, start))
         else:
             rows = refs[0].shape[0]
-            place = scalars["core"] if kind[0] == "held" else 1 - scalars["core"]
+            place = scalars.core if kind[0] == "held" else 1 - scalars.core
             parts.append((tuple(refs), 0, rows, (place * 2 + kind[1]) * rows))
         for part in parts:
             pending.append(part)
@@ -62,7 +63,9 @@
         start = pl.multiple_of(start, key_tile)
     rows = near[pl.ds(start, size), lanes]
     if far is not near:
-        rows = jnp.where(scalars["elsewhere"], far[pl.ds(start, size), lanes], rows)
+        rows = jnp.where(
+            scalars.elsewhere, far[pl.ds(start, size), lanes].astype(jnp.float32), rows.astype(jnp.float32)
+        )
     return rows
 
 
@@ -81,7 +84,7 @@
         length, live_count = length_ref[parent], live_ref[0]
     elif masks or finishes:
         info = refs.pop(0)[...]
-        local_branch, length, live_count = [jnp.max(info[number:number + 1]) for number in range(3)]
+        elsewhere, length, live_count = info[0:1] > 0, info[1:2], info[2:3]
     query_ref = refs.pop(0)
     spans = [(kind, [refs.pop(0) for _ in range(count)]) for kind, count in kinds]
     carries = not reads_numbers
@@ -91,19 +94,19 @@
         out_ref, held_ref, sems = refs
     else:
         total_ref, max_ref = refs.pop(0), refs.pop(0)
+    place = lax.axis_index("leaf")
     if form == "first":
         info_ref = refs.pop(0)
         row = lax.broadcasted_iota(jnp.int32, info_ref.shape, 0)
-        info_ref[...] = jnp.where(row == 0, local_branch, jnp.where(row == 1, length, live_count))
-    scalars = {}
+        other = (local_branch != lax.div(place, 2)).astype(jnp.int32)
+        info_ref[...] = jnp.where(row == 0, other, jnp.where(row == 1, length, live_count))
+    scalars = types.SimpleNamespace()
     if masks:
-        place = lax.axis_index("leaf")
-        scalars = dict(
-            local_branch=local_branch,
-            length=length,
-            core=lax.rem(place, 2),
-            elsewhere=local_branch != lax.div(place, 2),
-        )
+        scalars.length, scalars.core = length, lax.rem(place, 2)
+        if reads_numbers:
+            scalars.local_branch = local_branch
+        else:
+            scalars.elsewhere = elsewhere
         seen_ref = [listed for kind, listed in spans if kind == "root"][0][0]
     tiles = tiles_of(spans, scalars)
     row_count = query_ref.shape[0]
@@ -133,11 +136,11 @@
                 value_rows = load(part, lanes_at(KVH + k), scalars)
                 one_rows = jnp.ones_like(value_rows)
                 if part[3] is not None:
-                    used = lax.broadcasted_iota(jnp.int32, key_rows.shape, 0) < scalars["length"] - part[3]
+                    used = lax.broadcasted_iota(jnp.int32, key_rows.shape, 0) < scalars.length - part[3]
                     seen = seen_ref[:16, lanes_at(k)][:1].astype(jnp.float32)
-                    key_rows = jnp.where(used, key_rows.astype(jnp.float32), seen).astype(key_rows.dtype)
-                    value_rows = jnp.where(used, value_rows.astype(jnp.float32), 0.0).astype(key_rows.dtype)
-                    one_rows = jnp.where(used, 1.0, 0.0).astype(key_rows.dtype)
+                    key_rows = jnp.where(used, key_rows.astype(jnp.float32), seen).astype(query.dtype)
+                    value_rows = jnp.where(used, value_rows.astype(jnp.float32), 0.0).astype(query.dtype)
+                    one_rows = jnp.where(used, 1.0, 0.0).astype(query.dtype)
                 keys.append(key_rows)
                 values.append(value_rows)
                 ones.append(one_rows)
@@ -331,18 +334,18 @@
     near_side_swapped = swap(near_side)
     far_side_swapped = swap(far_side)
     state = attend("middle", (info,), kept, [
+        ("root", [near_side, far_side, near_side_swapped, far_side_swapped]),
         (("held", 0), [low, low_side]),
         (("swapped", 0), [low_swapped, low_side_swapped]),
-        ("root", [near_side, far_side, near_side_swapped, far_side_swapped]),
     ], state)
 
     cross_own_swapped = swap(cross_own)
     high_side_swapped = swap(high_side)
     cross_side_swapped = swap(cross_side)
     state = attend("middle", (info,), kept, [
+        ("root", [cross_own, cross_own_swapped]),
         (("held", 1), [high, high_side]),
         (("swapped", 1), [high_swapped, high_side_swapped]),
-        ("root", [cross_own, cross_own_swapped]),
     ], state)
     return attend("last", (info,), kept, [("root", [cross_side, cross_side_swapped])], state)
 

time: 53.6 us -> 53 us (0.989)
    pallas_call x5, Pallas kernels: 18.8 us -> 18.3 us  [attend(): pl.pallas_call(functools.partial(attend_kernel, tuple(((kind, len(listed)...]
where the time goes in v5:
time: 53 us; the launch traced here: 52.9 us
  Pallas kernels  19.9 us (38%)
  starting transfers between devices  17.8 us (34%)
  waiting for transfers between devices  13 us (25%)
  between operations  1.61 us (3%)
  local copies, waits for them, and re-layouts  0.65 us (1%)
    pallas_call x5, Pallas kernels, attend(): pl.pallas_call(functools.partial(attend_kernel, tuple(((kind, len(listed)...  18.3 us
    ppermute x1, waiting for transfers between devices, exchanged_body(): near_own = lax.ppermute(root_kv, 'branch', near)  4.98 us
    ppermute x1, starting transfers between devices, exchanged_body(): far_own = lax.ppermute(root_kv, 'branch', far)  3.6 us
    ppermute x1, starting transfers between devices, exchanged_body(): cross_own = lax.ppermute(pick(own, far_own), 'branch', cross)  2.61 us
    ppermute x1, starting transfers between devices, exchanged_body(): side = lax.ppermute(root_kv, 'leaf', across)  2.48 us
    ppermute x1, starting transfers between devices, exchanged_body(): high_side = lax.ppermute(high, 'leaf', across)  2.2 us
    ppermute x12, starting transfers between devices, swap(): return lax.ppermute(rows, 'leaf', beside)  2.04 us
    ppermute x1, waiting for transfers between devices, exchanged_body(): high_side = lax.ppermute(high, 'leaf', across)  1.96 us
  transfers between devices with their start and end apart: 21, of which 6 were waited for; matrix products, arithmetic and copies ran while one was open for 0% of the time, Pallas kernels for 33%

profile of v5, /device:TPU:0, one launch (start us, length us, event | category | flops | bytes accessed | tf_op | source)
XLA Modules:
  0.0 52.9 jit_solution(1247784877119197875)
XLA Ops:
  0.0 0.5 collective-permute-start
  0.5 2.5 %collective-permute-start.1 = (bf16[128,1024]{1,0:T(8,128)(2,1)}, bf16[128,1024]{1,0:T(8,128)(2,1)S(1)}, u32[]{:S(2)}, u32[]{:S(2)}) collective-permute-start(bf16[128,1024]{1,0:T(8,128)(2,1)} %refs_2_.2), channel_id=1, source_target_pairs={{0,2},{1,3},{2,0},{3,1},{4,6},{5,7},{6,4},{7,5},{8,10},{9,11},{10,... | collective-permute-start | bytes 786440 | tf_op jit(solution)/shard_map/ppermute | solution.py:313
  3.0 3.6 %collective-permute-start.2 = (bf16[128,1024]{1,0:T(8,128)(2,1)}, bf16[128,1024]{1,0:T(8,128)(2,1)S(1)}, u32[]{:S(2)}, u32[]{:S(2)}) collective-permute-start(bf16[128,1024]{1,0:T(8,128)(2,1)} %refs_2_.2), channel_id=1, source_target_pairs={{0,12},{4,8},{8,4},{12,0},{1,13},{5,9},{9,5},{13,1},{2,14},{6,10},... | collective-permute-start | bytes 786440 | tf_op jit(solution)/shard_map/ppermute | solution.py:311
  6.6 1.5 %shard_map.73 = (bf16[128,4096]{1,0:T(8,128)(2,1)S(1)}, bf16[128,1024]{1,0:T(8,128)(2,1)S(1)}, bf16[128,1024]{1,0:T(8,128)(2,1)S(1)}, bf16[128,1024]{1,0:T(8,128)(2,1)S(1)}, bf16[128,1024]{1,0:T(8,128)(2,1)S(1)}) custom-call(bf16[128,4096]{1,0:T(8,128)(2,1)} %refs_0_.2, bf16[128,1024]{1,0:T(8,128)(2,1)} %refs_1_.2, bf16[128,1024]{1,0:T(8,128)(2,1)} %refs_2_.2, ...), custom_call_target="tpu_custom_call" | custom-call | tf_op jit(solution)/shard_map/pallas_call | solution.py:259
  8.1 0.6 %collective-permute-start.14 = (bf16[128,1024]{1,0:T(8,128)(2,1)S(1)}, bf16[128,1024]{1,0:T(8,128)(2,1)S(1)}, u32[]{:S(2)}, u32[]{:S(2)}) collective-permute-start(bf16[128,1024]{1,0:T(8,128)(2,1)S(1)} %get-tuple-element.24.refs_6_), channel_id=1, source_target_pairs={{0,2},{1,3},{2,0},{3,1},{4,6},{5,7},{6,4},{7,5},{8,10},{9,11},{10,... | collective-permute-start | bytes 786440 | tf_op jit(solution)/shard_map/ppermute | solution.py:316
  8.7 1.4 %collective-permute-done.1.end_ref.refs_1_ = bf16[128,1024]{1,0:T(8,128)(2,1)S(1)} collective-permute-done((bf16[128,1024]{1,0:T(8,128)(2,1)}, bf16[128,1024]{1,0:T(8,128)(2,1)S(1)}, u32[]{:S(2)}, u32[]{:S(2)}) %collective-permute-start.1) | collective-permute-done | bytes 262176 | tf_op jit(solution)/shard_map/ppermute | solution.py:313
  10.2 2.2 %collective-permute-start.8 = (bf16[128,1024]{1,0:T(8,128)(2,1)S(1)}, bf16[128,1024]{1,0:T(8,128)(2,1)S(1)}, u32[]{:S(2)}, u32[]{:S(2)}) collective-permute-start(bf16[128,1024]{1,0:T(8,128)(2,1)S(1)} %get-tuple-element.23.refs_4_), channel_id=1, source_target_pairs={{0,2},{1,3},{2,0},{3,1},{4,6},{5,7},{6,4},{7,5},{8,10},{9,11},{10,... | collective-permute-start | bytes 786440 | tf_op jit(solution)/shard_map/ppermute | solution.py:317
  12.4 1.9 %collective-permute-done.2.middle_ref.refs_3_ = bf16[128,1024]{1,0:T(8,128)(2,1)S(1)} collective-permute-done((bf16[128,1024]{1,0:T(8,128)(2,1)}, bf16[128,1024]{1,0:T(8,128)(2,1)S(1)}, u32[]{:S(2)}, u32[]{:S(2)}) %collective-permute-start.2) | collective-permute-done | bytes 262176 | tf_op jit(solution)/shard_map/ppermute | solution.py:311
  14.3 5.0 %collective-permute-done.17.refs_2_ = bf16[128,1024]{1,0:T(8,128)(2,1)S(1)} collective-permute-done((bf16[128,1024]{1,0:T(8,128)(2,1)}, bf16[128,1024]{1,0:T(8,128)(2,1)S(1)}, u32[]{:S(2)}, u32[]{:S(2)}) %collective-permute-start.17) | collective-permute-done | bytes 262176 | tf_op jit(solution)/shard_map/ppermute | solution.py:312
  19.3 0.5 %collective-permute-start.3 = (bf16[128,1024]{1,0:T(8,128)(2,1)S(1)}, bf16[128,1024]{1,0:T(8,128)(2,1)S(1)}, u32[]{:S(2)}, u32[]{:S(2)}) collective-permute-start(bf16[128,1024]{1,0:T(8,128)(2,1)S(1)} %collective-permute-done.2.middle_ref.refs_3_), channel_id=1, source_target_pairs={{0,2},{1,3},{2,0},{3,1},{4,6},{5,7},{6,4},{7,5},{8,10},{9,11},{10,... | collective-permute-start | bytes 786440 | tf_op jit(solution)/shard_map/ppermute | solution.py:323
  20.0 2.0 %collective-permute-done.8.refs_5_ = bf16[128,1024]{1,0:T(8,128)(2,1)S(1)} collective-permute-done((bf16[128,1024]{1,0:T(8,128)(2,1)S(1)}, bf16[128,1024]{1,0:T(8,128)(2,1)S(1)}, u32[]{:S(2)}, u32[]{:S(2)}) %collective-permute-start.8) | collective-permute-done | bytes 262176 | tf_op jit(solution)/shard_map/ppermute | solution.py:317
  22.0 1.7 %collective-permute-start.11 = (bf16[128,1024]{1,0:T(8,128)(2,1)S(1)}, bf16[128,1024]{1,0:T(8,128)(2,1)S(1)}, u32[]{:S(2)}, u32[]{:S(2)}) collective-permute-start(bf16[128,1024]{1,0:T(8,128)(2,1)S(1)} %collective-permute-done.1.end_ref.refs_1_), channel_id=1, source_target_pairs={{0,4},{4,0},{8,12},{12,8},{1,5},{5,1},{9,13},{13,9},{2,6},{6,2},{1... | collective-permute-start | bytes 786440 | tf_op jit(solution)/shard_map/ppermute | solution.py:322
  23.8 2.6 %collective-permute-start.6 = (bf16[128,1024]{1,0:T(8,128)(2,1)S(1)}, bf16[128,1024]{1,0:T(8,128)(2,1)S(1)}, u32[]{:S(2)}, u32[]{:S(2)}) collective-permute-start(bf16[128,1024]{1,0:T(8,128)(2,1)S(1)} %shard_map.76), channel_id=1, source_target_pairs={{4,0},{8,12},{12,4},{0,8},{5,1},{9,13},{13,5},{1,9},{6,2},{10,14},... | collective-permute-start | bytes 786440 | tf_op jit(solution)/shard_map/ppermute | solution.py:324
  26.4 1.5 %collective-permute-done.3.middle_ref.refs_3_ = bf16[128,1024]{1,0:T(8,128)(2,1)S(1)} collective-permute-done((bf16[128,1024]{1,0:T(8,128)(2,1)S(1)}, bf16[128,1024]{1,0:T(8,128)(2,1)S(1)}, u32[]{:S(2)}, u32[]{:S(2)}) %collective-permute-start.3) | collective-permute-done | bytes 262176 | tf_op jit(solution)/shard_map/ppermute | solution.py:323
  28.0 1.9 %collective-permute-start.4 = (bf16[128,1024]{1,0:T(8,128)(2,1)S(1)}, bf16[128,1024]{1,0:T(8,128)(2,1)S(1)}, u32[]{:S(2)}, u32[]{:S(2)}) collective-permute-start(bf16[128,1024]{1,0:T(8,128)(2,1)S(1)} %shard_map.75), channel_id=1, source_target_pairs={{4,0},{8,12},{12,4},{0,8},{5,1},{9,13},{13,5},{1,9},{6,2},{10,14},... | collective-permute-start | bytes 786440 | tf_op jit(solution)/shard_map/ppermute | solution.py:333
  29.9 1.2 %collective-permute-done.11.refs_2_ = bf16[128,1024]{1,0:T(8,128)(2,1)S(1)} collective-permute-done((bf16[128,1024]{1,0:T(8,128)(2,1)S(1)}, bf16[128,1024]{1,0:T(8,128)(2,1)S(1)}, u32[]{:S(2)}, u32[]{:S(2)}) %collective-permute-start.11) | collective-permute-done | bytes 262176 | tf_op jit(solution)/shard_map/ppermute | solution.py:322
  32.5 0.6 %copy-done = s32[8]{0:T(128)S(1)} copy-done((s32[8]{0:T(128)S(1)}, s32[8]{0:T(128)}, u32[]{:S(2)}) %copy-start) | copy-done | bytes 56
  33.1 3.3 %shard_map.74 = (f32[4096,256]{1,0:T(8,128)S(1)}, f32[4096,128]{1,0:T(8,128)S(1)}, s32[8,128]{1,0:T(8,128)S(1)}) custom-call(s32[1]{0:T(128)S(6)} %copy.21.refs_0_, s32[8]{0:T(128)S(1)} %copy-done, s32[1]{0:T(128)S(6)} %copy.20.refs_2_, bf16[128,4096]{1,0:T(8,128)(2,1)S(1)} %get-tuple-element.19.refs_3_.refs_0_.refs_1_, ...), custom_call_target="tpu_custom_call" | custom-call | flops 805306368 | bytes 4194304 | tf_op jit(solution)/shard_map/pallas_call | solution.py:222
  36.5 0.6 %collective-permute-start.9 = (bf16[128,1024]{1,0:T(8,128)(2,1)S(1)}, bf16[128,1024]{1,0:T(8,128)(2,1)S(1)}, u32[]{:S(2)}, u32[]{:S(2)}) collective-permute-start(bf16[128,1024]{1,0:T(8,128)(2,1)S(1)} %get-tuple-element.23.refs_4_), channel_id=1, source_target_pairs={{0,1},{1,0},{2,3},{3,2},{4,5},{5,4},{6,7},{7,6},{8,9},{9,8},{10,11... | collective-permute-start | bytes 786440 | tf_op jit(solution)/shard_map/ppermute | solution.py:309
  37.1 0.4 collective-permute-start.7
  37.6 4.2 %shard_map.77 = (f32[4096,256]{1,0:T(8,128)S(1)}, f32[4096,128]{1,0:T(8,128)S(1)}) custom-call(bf16[128,4096]{1,0:T(8,128)(2,1)S(1)} %get-tuple-element.19.refs_3_.refs_0_.refs_1_, bf16[128,1024]{1,0:T(8,128)(2,1)S(1)} %collective-permute-done.1.end_ref.refs_1_, ...), custom_call_target="tpu_custom_call", output_to_operand_aliasing={{0}: (7, {}), {1}: (8, {})} | custom-call | flops 1610612736 | bytes 4194304 | tf_op jit(solution)/shard_map/pallas_call | solution.py:222
  41.9 4.4 %shard_map.78 = (f32[4096,256]{1,0:T(8,128)S(1)}, f32[4096,128]{1,0:T(8,128)S(1)}) custom-call(s32[8,128]{1,0:T(8,128)S(1)} %get-tuple-element.22.refs_0_, bf16[128,4096]{1,0:T(8,128)(2,1)S(1)} %get-tuple-element.19.refs_3_.refs_0_.refs_1_, bf16[128,1024]{1,0:T(8,128)(2,1)S(1)} %collective-permute-done.11.refs_2_, ...), custom_call_target="tpu_custom_call", output_to_operand_aliasing={{0}: (10, {}), {1}: (11, {})} | custom-call | flops 2147483648 | bytes 4194304 | tf_op jit(solution)/shard_map/pallas_call | solution.py:222
  46.4 3.7 %shard_map.79 = (f32[4096,256]{1,0:T(8,128)S(1)}, f32[4096,128]{1,0:T(8,128)S(1)}) custom-call(s32[8,128]{1,0:T(8,128)S(1)} %get-tuple-element.22.refs_0_, bf16[128,4096]{1,0:T(8,128)(2,1)S(1)} %get-tuple-element.19.refs_3_.refs_0_.refs_1_, bf16[128,1024]{1,0:T(8,128)(2,1)S(1)} %collective-permute-done.6.refs_2_, ...), custom_call_target="tpu_custom_call", output_to_operand_aliasing={{0}: (8, {}), {1}: (9, {})} | custom-call | flops 1610612736 | bytes 4194304 | tf_op jit(solution)/shard_map/pallas_call | solution.py:222
  50.1 2.7 %shard_map.80 = bf16[128,4096]{1,0:T(8,128)(2,1)} custom-call(s32[8,128]{1,0:T(8,128)S(1)} %get-tuple-element.22.refs_0_, bf16[128,4096]{1,0:T(8,128)(2,1)S(1)} %get-tuple-element.19.refs_3_.refs_0_.refs_1_, bf16[128,1024]{1,0:T(8,128)(2,1)S(1)} %collective-permute-done.4.refs_2_, bf16[128,1024]{1,0:T(8,128)(2,1)S(1)} %collective-permute-done.5.refs_3_, ...), custom_call_target="tpu_custom_call" | custom-call | flops 536870912 | bytes 4194304 | tf_op jit(solution)/shard_map/pallas_call | solution.py:222
  (28 shorter events, 0.6 us)
Async XLA Ops:
  0.0 8.7 %collective-permute-start = (bf16[128,1024]{1,0:T(8,128)(2,1)}, bf16[128,1024]{1,0:T(8,128)(2,1)S(1)}, u32[]{:S(2)}, u32[]{:S(2)}) collective-permute-start(bf16[128,1024]{1,0:T(8,128)(2,1)} %refs_2_.2), channel_id=1, source_target_pairs={{0,1},{1,0},{2,3},{3,2},{4,5},{5,4},{6,7},{7,6},{8,9},{9,8},{10,11... | collective-permute-start | bytes 786440 | tf_op jit(solution)/shard_map/ppermute | solution.py:309
  0.5 9.7 %collective-permute-start.1 = (bf16[128,1024]{1,0:T(8,128)(2,1)}, bf16[128,1024]{1,0:T(8,128)(2,1)S(1)}, u32[]{:S(2)}, u32[]{:S(2)}) collective-permute-start(bf16[128,1024]{1,0:T(8,128)(2,1)} %refs_2_.2), channel_id=1, source_target_pairs={{0,2},{1,3},{2,0},{3,1},{4,6},{5,7},{6,4},{7,5},{8,10},{9,11},{10,... | collective-permute-start | bytes 786440 | tf_op jit(solution)/shard_map/ppermute | solution.py:313
  3.0 11.3 %collective-permute-start.2 = (bf16[128,1024]{1,0:T(8,128)(2,1)}, bf16[128,1024]{1,0:T(8,128)(2,1)S(1)}, u32[]{:S(2)}, u32[]{:S(2)}) collective-permute-start(bf16[128,1024]{1,0:T(8,128)(2,1)} %refs_2_.2), channel_id=1, source_target_pairs={{0,12},{4,8},{8,4},{12,0},{1,13},{5,9},{9,5},{13,1},{2,14},{6,10},... | collective-permute-start | bytes 786440 | tf_op jit(solution)/shard_map/ppermute | solution.py:311
  6.6 12.7 %collective-permute-start.17 = (bf16[128,1024]{1,0:T(8,128)(2,1)}, bf16[128,1024]{1,0:T(8,128)(2,1)S(1)}, u32[]{:S(2)}, u32[]{:S(2)}) collective-permute-start(bf16[128,1024]{1,0:T(8,128)(2,1)} %refs_2_.2), channel_id=1, source_target_pairs={{0,4},{4,0},{8,12},{12,8},{1,5},{5,1},{9,13},{13,9},{2,6},{6,2},{1... | collective-permute-start | bytes 786440 | tf_op jit(solution)/shard_map/ppermute | solution.py:312
  8.1 11.1 %collective-permute-start.14 = (bf16[128,1024]{1,0:T(8,128)(2,1)S(1)}, bf16[128,1024]{1,0:T(8,128)(2,1)S(1)}, u32[]{:S(2)}, u32[]{:S(2)}) collective-permute-start(bf16[128,1024]{1,0:T(8,128)(2,1)S(1)} %get-tuple-element.24.refs_6_), channel_id=1, source_target_pairs={{0,2},{1,3},{2,0},{3,1},{4,6},{5,7},{6,4},{7,5},{8,10},{9,11},{10,... | collective-permute-start | bytes 786440 | tf_op jit(solution)/shard_map/ppermute | solution.py:316
  8.7 11.1 %collective-permute-start.15 = (bf16[128,1024]{1,0:T(8,128)(2,1)S(1)}, bf16[128,1024]{1,0:T(8,128)(2,1)S(1)}, u32[]{:S(2)}, u32[]{:S(2)}) collective-permute-start(bf16[128,1024]{1,0:T(8,128)(2,1)S(1)} %get-tuple-element.24.refs_6_), channel_id=1, source_target_pairs={{0,1},{1,0},{2,3},{3,2},{4,5},{5,4},{6,7},{7,6},{8,9},{9,8},{10,11... | collective-permute-start | bytes 786440 | tf_op jit(solution)/shard_map/ppermute | solution.py:309
  10.2 11.8 %collective-permute-start.8 = (bf16[128,1024]{1,0:T(8,128)(2,1)S(1)}, bf16[128,1024]{1,0:T(8,128)(2,1)S(1)}, u32[]{:S(2)}, u32[]{:S(2)}) collective-permute-start(bf16[128,1024]{1,0:T(8,128)(2,1)S(1)} %get-tuple-element.23.refs_4_), channel_id=1, source_target_pairs={{0,2},{1,3},{2,0},{3,1},{4,6},{5,7},{6,4},{7,5},{8,10},{9,11},{10,... | collective-permute-start | bytes 786440 | tf_op jit(solution)/shard_map/ppermute | solution.py:317
  14.3 9.5 %collective-permute-start.18 = (bf16[128,1024]{1,0:T(8,128)(2,1)S(1)}, bf16[128,1024]{1,0:T(8,128)(2,1)S(1)}, u32[]{:S(2)}, u32[]{:S(2)}) collective-permute-start(bf16[128,1024]{1,0:T(8,128)(2,1)S(1)} %collective-permute-done.1.end_ref.refs_1_), channel_id=1, source_target_pairs={{0,1},{1,0},{2,3},{3,2},{4,5},{5,4},{6,7},{7,6},{8,9},{9,8},{10,11... | collective-permute-start | bytes 786440 | tf_op jit(solution)/shard_map/ppermute | solution.py:309
  19.2 4.6 %collective-permute-start.20 = (bf16[128,1024]{1,0:T(8,128)(2,1)S(1)}, bf16[128,1024]{1,0:T(8,128)(2,1)S(1)}, u32[]{:S(2)}, u32[]{:S(2)}) collective-permute-start(bf16[128,1024]{1,0:T(8,128)(2,1)S(1)} %collective-permute-done.2.middle_ref.refs_3_), channel_id=1, source_target_pairs={{0,1},{1,0},{2,3},{3,2},{4,5},{5,4},{6,7},{7,6},{8,9},{9,8},{10,11... | collective-permute-start | bytes 786440 | tf_op jit(solution)/shard_map/ppermute | solution.py:309
  19.3 8.7 %collective-permute-start.3 = (bf16[128,1024]{1,0:T(8,128)(2,1)S(1)}, bf16[128,1024]{1,0:T(8,128)(2,1)S(1)}, u32[]{:S(2)}, u32[]{:S(2)}) collective-permute-start(bf16[128,1024]{1,0:T(8,128)(2,1)S(1)} %collective-permute-done.2.middle_ref.refs_3_), channel_id=1, source_target_pairs={{0,2},{1,3},{2,0},{3,1},{4,6},{5,7},{6,4},{7,5},{8,10},{9,11},{10,... | collective-permute-start | bytes 786440 | tf_op jit(solution)/shard_map/ppermute | solution.py:323
  19.8 8.2 %collective-permute-start.19 = (bf16[128,1024]{1,0:T(8,128)(2,1)S(1)}, bf16[128,1024]{1,0:T(8,128)(2,1)S(1)}, u32[]{:S(2)}, u32[]{:S(2)}) collective-permute-start(bf16[128,1024]{1,0:T(8,128)(2,1)S(1)} %collective-permute-done.17.refs_2_), channel_id=1, source_target_pairs={{0,1},{1,0},{2,3},{3,2},{4,5},{5,4},{6,7},{7,6},{8,9},{9,8},{10,11... | collective-permute-start | bytes 786440 | tf_op jit(solution)/shard_map/ppermute | solution.py:309
  22.0 9.2 %collective-permute-start.11 = (bf16[128,1024]{1,0:T(8,128)(2,1)S(1)}, bf16[128,1024]{1,0:T(8,128)(2,1)S(1)}, u32[]{:S(2)}, u32[]{:S(2)}) collective-permute-start(bf16[128,1024]{1,0:T(8,128)(2,1)S(1)} %collective-permute-done.1.end_ref.refs_1_), channel_id=1, source_target_pairs={{0,4},{4,0},{8,12},{12,8},{1,5},{5,1},{9,13},{13,9},{2,6},{6,2},{1... | collective-permute-start | bytes 786440 | tf_op jit(solution)/shard_map/ppermute | solution.py:322
  23.7 12.7 %collective-permute-start.16 = (bf16[128,1024]{1,0:T(8,128)(2,1)S(1)}, bf16[128,1024]{1,0:T(8,128)(2,1)S(1)}, u32[]{:S(2)}, u32[]{:S(2)}) collective-permute-start(bf16[128,1024]{1,0:T(8,128)(2,1)S(1)} %collective-permute-done.14.refs_7_), channel_id=1, source_target_pairs={{0,1},{1,0},{2,3},{3,2},{4,5},{5,4},{6,7},{7,6},{8,9},{9,8},{10,11... | collective-permute-start | bytes 786440 | tf_op jit(solution)/shard_map/ppermute | solution.py:309
  23.8 13.2 %collective-permute-start.6 = (bf16[128,1024]{1,0:T(8,128)(2,1)S(1)}, bf16[128,1024]{1,0:T(8,128)(2,1)S(1)}, u32[]{:S(2)}, u32[]{:S(2)}) collective-permute-start(bf16[128,1024]{1,0:T(8,128)(2,1)S(1)} %shard_map.76), channel_id=1, source_target_pairs={{4,0},{8,12},{12,4},{0,8},{5,1},{9,13},{13,5},{1,9},{6,2},{10,14},... | collective-permute-start | bytes 786440 | tf_op jit(solution)/shard_map/ppermute | solution.py:324
  28.0 9.2 %collective-permute-start.13 = (bf16[128,1024]{1,0:T(8,128)(2,1)S(1)}, bf16[128,1024]{1,0:T(8,128)(2,1)S(1)}, u32[]{:S(2)}, u32[]{:S(2)}) collective-permute-start(bf16[128,1024]{1,0:T(8,128)(2,1)S(1)} %collective-permute-done.3.middle_ref.refs_3_), channel_id=1, source_target_pairs={{0,1},{1,0},{2,3},{3,2},{4,5},{5,4},{6,7},{7,6},{8,9},{9,8},{10,11... | collective-permute-start | bytes 786440 | tf_op jit(solution)/shard_map/ppermute | solution.py:309
  28.0 13.8 %collective-permute-start.4 = (bf16[128,1024]{1,0:T(8,128)(2,1)S(1)}, bf16[128,1024]{1,0:T(8,128)(2,1)S(1)}, u32[]{:S(2)}, u32[]{:S(2)}) collective-permute-start(bf16[128,1024]{1,0:T(8,128)(2,1)S(1)} %shard_map.75), channel_id=1, source_target_pairs={{4,0},{8,12},{12,4},{0,8},{5,1},{9,13},{13,5},{1,9},{6,2},{10,14},... | collective-permute-start | bytes 786440 | tf_op jit(solution)/shard_map/ppermute | solution.py:333
  31.1 10.8 %collective-permute-start.12 = (bf16[128,1024]{1,0:T(8,128)(2,1)S(1)}, bf16[128,1024]{1,0:T(8,128)(2,1)S(1)}, u32[]{:S(2)}, u32[]{:S(2)}) collective-permute-start(bf16[128,1024]{1,0:T(8,128)(2,1)S(1)} %collective-permute-done.11.refs_2_), channel_id=1, source_target_pairs={{0,1},{1,0},{2,3},{3,2},{4,5},{5,4},{6,7},{7,6},{8,9},{9,8},{10,11... | collective-permute-start | bytes 786440 | tf_op jit(solution)/shard_map/ppermute | solution.py:309
  32.5 0.7 %copy-start = (s32[8]{0:T(128)S(1)}, s32[8]{0:T(128)}, u32[]{:S(2)}) copy-start(s32[8]{0:T(128)} %refs_1_.3) | copy-start | bytes 100
  36.5 9.9 %collective-permute-start.9 = (bf16[128,1024]{1,0:T(8,128)(2,1)S(1)}, bf16[128,1024]{1,0:T(8,128)(2,1)S(1)}, u32[]{:S(2)}, u32[]{:S(2)}) collective-permute-start(bf16[128,1024]{1,0:T(8,128)(2,1)S(1)} %get-tuple-element.23.refs_4_), channel_id=1, source_target_pairs={{0,1},{1,0},{2,3},{3,2},{4,5},{5,4},{6,7},{7,6},{8,9},{9,8},{10,11... | collective-permute-start | bytes 786440 | tf_op jit(solution)/shard_map/ppermute | solution.py:309
  37.0 9.3 %collective-permute-start.10 = (bf16[128,1024]{1,0:T(8,128)(2,1)S(1)}, bf16[128,1024]{1,0:T(8,128)(2,1)S(1)}, u32[]{:S(2)}, u32[]{:S(2)}) collective-permute-start(bf16[128,1024]{1,0:T(8,128)(2,1)S(1)} %collective-permute-done.8.refs_5_), channel_id=1, source_target_pairs={{0,1},{1,0},{2,3},{3,2},{4,5},{5,4},{6,7},{7,6},{8,9},{9,8},{10,11... | collective-permute-start | bytes 786440 | tf_op jit(solution)/shard_map/ppermute | solution.py:309
  37.1 9.2 %collective-permute-start.7 = (bf16[128,1024]{1,0:T(8,128)(2,1)S(1)}, bf16[128,1024]{1,0:T(8,128)(2,1)S(1)}, u32[]{:S(2)}, u32[]{:S(2)}) collective-permute-start(bf16[128,1024]{1,0:T(8,128)(2,1)S(1)} %collective-permute-done.6.refs_2_), channel_id=1, source_target_pairs={{0,1},{1,0},{2,3},{3,2},{4,5},{5,4},{6,7},{7,6},{8,9},{9,8},{10,11... | collective-permute-start | bytes 786440 | tf_op jit(solution)/shard_map/ppermute | solution.py:309
  41.8 8.3 %collective-permute-start.5 = (bf16[128,1024]{1,0:T(8,128)(2,1)S(1)}, bf16[128,1024]{1,0:T(8,128)(2,1)S(1)}, u32[]{:S(2)}, u32[]{:S(2)}) collective-permute-start(bf16[128,1024]{1,0:T(8,128)(2,1)S(1)} %collective-permute-done.4.refs_2_), channel_id=1, source_target_pairs={{0,1},{1,0},{2,3},{3,2},{4,5},{5,4},{6,7},{7,6},{8,9},{9,8},{10,11... | collective-permute-start | bytes 786440 | tf_op jit(solution)/shard_map/ppermute | solution.py:309
